TPU v7x, 512 devices: a whole 4x8x8 slice. The times are simulated.
512 devices in a mesh: dp: 2 (over z_hi), ctx: 32 (over z_lo, y), tp: 8 (over x, core).
Axes of the slice: x: 4, y: 8, z: 8 (z_hi: 2, z_lo: 4; z = z_hi * 4 + z_lo), core: 2. Of those that a mesh axis runs over, the one named last changes fastest.
Arguments:
- left_stream: bfloat16 [2, 4096, 4096], P('dp', 'ctx', 'tp'), may hold values from -6 to 6
- outer_gate: bfloat16 [2, 4096, 4096], P('dp', 'ctx', 'tp'), may hold values from -6 to 6
- value_stream: bfloat16 [2, 4096, 4096], P('dp', 'ctx', 'tp'), may hold values from -6 to 6
- residual: bfloat16 [2, 4096, 4096], P('dp', 'ctx', 'tp'), may hold values from -36 to 36
- long_filter: float32 [256, 128], P('tp'), may hold values from -2 to 2
- skip_weight: float32 [4096], P('tp'), may hold values from -1 to 1
- norm_gain: float32 [4096], P('tp'), may hold values from 0.1 to 1.9
- normed_grad: bfloat16 [2, 4096, 4096], P('dp', 'ctx', 'tp'), may hold values from -6 to 6
- attn_queries: bfloat16 [2, 4096, 4096], P('dp', 'ctx', 'tp'), may hold values from -6 to 6
- attn_keys: bfloat16 [2, 4096, 4096], P('dp', 'ctx', 'tp'), may hold values from -6 to 6
- attn_values: bfloat16 [2, 4096, 4096], P('dp', 'ctx', 'tp'), may hold values from -6 to 6
- attended_grad: bfloat16 [2, 4096, 4096], P('dp', 'ctx', 'tp'), may hold values from -6 to 6
Outputs:
- normed: bfloat16 [2, 4096, 4096], P('dp', 'ctx', 'tp')
- grad_left: bfloat16 [2, 4096, 4096], P('dp', 'ctx', 'tp')
- grad_outer: bfloat16 [2, 4096, 4096], P('dp', 'ctx', 'tp')
- grad_value: bfloat16 [2, 4096, 4096], P('dp', 'ctx', 'tp')
- grad_residual: bfloat16 [2, 4096, 4096], P('dp', 'ctx', 'tp')
- grad_filter: float32 [256, 128], P('tp')
- grad_skip: float32 [4096], P('tp')
- grad_gain: float32 [4096], P('tp')
- attended: bfloat16 [2, 4096, 4096], P('dp', 'ctx', 'tp')
- grad_queries: bfloat16 [2, 4096, 4096], P('dp', 'ctx', 'tp')
- grad_keys: bfloat16 [2, 4096, 4096], P('dp', 'ctx', 'tp')
- grad_values: bfloat16 [2, 4096, 4096], P('dp', 'ctx', 'tp')
All inputs are finite; a program needn't handle non-finite values.
Results may differ from a plain program's by a relative error of at most 0.024.
Values may be sent and summed in bfloat16 or wider, within the bound.
A program may use at most 128 MiB of HBM per device.

v0:
```python
import jax
import jax.numpy as jnp
from jax import lax
from jax.sharding import PartitionSpec as P

HEAD_DIM = 128


def passed_along(value, axis, steps):
    count = lax.axis_size(axis)
    initial, last = (max(0, -steps), min(count, count - steps))
    return lax.ppermute(value, axis, [(source, source + steps) for source in range(initial, last)])


def toeplitz(taps_rows, rows):
    groups, length = taps_rows.shape
    width = rows + length - 1
    padded = jnp.pad(taps_rows, ((0, 0), (0, width + 1 - length)))
    tiled = jnp.tile(padded, (1, rows))[:, : rows * width]
    return tiled.reshape(groups, rows, width)


def diagonals(matrix, length):
    groups, rows, width = matrix.shape
    flat = jnp.pad(matrix.reshape(groups, rows * width), ((0, 0), (0, rows)))
    return flat.reshape(groups, rows, width + 1)[:, :, :length]


def scores_block(query_rows, key_block, scale):
    return (
        jnp.einsum("rhd,khd->hrk", query_rows, key_block, preferred_element_type=jnp.float32)
        * scale
    )


def key_block_at(key_all, value_all, number, block, positions):
    begin = number * block
    keys_here = lax.dynamic_slice_in_dim(key_all, begin, block, 0)
    values_here = lax.dynamic_slice_in_dim(value_all, begin, block, 0)
    key_pos = begin + jnp.arange(block, dtype=jnp.int32)
    allowed = key_pos[None, :] <= positions[:, None]
    return (keys_here, values_here, allowed)


def attend_rows(query_rows, first_pos, key_all, value_all, block, scale):
    count_rows = query_rows.shape[0]
    heads_here = query_rows.shape[1]
    positions = first_pos + jnp.arange(count_rows, dtype=jnp.int32)
    needed = (first_pos + count_rows - 1) // block + 1

    def first_pass(number, carry):
        running, total = carry
        keys_here, values_here, allowed = key_block_at(key_all, value_all, number, block, positions)
        scores = jnp.where(allowed[None], scores_block(query_rows, keys_here, scale), -jnp.inf)
        newest = jnp.maximum(running, jnp.max(scores, axis=2))
        total = total * jnp.exp(running - newest) + jnp.sum(
            jnp.exp(scores - newest[:, :, None]), axis=2
        )
        return (newest, total)

    start_carry = (
        jnp.full((heads_here, count_rows), -jnp.inf, jnp.float32),
        jnp.zeros((heads_here, count_rows), jnp.float32),
    )
    running, total = lax.fori_loop(0, needed, first_pass, start_carry)
    log_norm = running + jnp.log(total)

    def second_pass(number, output):
        keys_here, values_here, allowed = key_block_at(key_all, value_all, number, block, positions)
        scores = jnp.where(allowed[None], scores_block(query_rows, keys_here, scale), -jnp.inf)
        weights = jnp.exp(scores - log_norm[:, :, None]).astype(jnp.bfloat16)
        return output + jnp.einsum(
            "hrk,khd->rhd", weights, values_here, preferred_element_type=jnp.float32
        )

    output = lax.fori_loop(0, needed, second_pass, jnp.zeros(query_rows.shape, jnp.float32))
    return (output, log_norm)


def shards(
    left_stream,
    outer_gate,
    value_stream,
    residual,
    long_filter,
    skip_weight,
    norm_gain,
    normed_grad,
    attn_queries,
    attn_keys,
    attn_values,
    attended_grad,
):
    rows = left_stream.shape[1]
    channels = left_stream.shape[2]
    groups = long_filter.shape[0]
    taps = long_filter.shape[1]
    per_group = channels // groups
    width = channels * lax.axis_size("tp")
    heads_here = attn_queries.shape[2] // HEAD_DIM
    scale = HEAD_DIM ** (-0.5)
    key_all, value_all = (
        lax.all_gather(attn_keys[0], "ctx", axis=0, tiled=True),
        lax.all_gather(attn_values[0], "ctx", axis=0, tiled=True),
    )
    seq_len = key_all.shape[0]
    key_all = key_all.reshape(seq_len, heads_here, HEAD_DIM)
    value_all = value_all.reshape(seq_len, heads_here, HEAD_DIM)
    left_values = left_stream[0].astype(jnp.float32)
    value_values = value_stream[0].astype(jnp.float32)
    gate_values = outer_gate[0].astype(jnp.float32)
    product = (left_values * value_values).astype(jnp.bfloat16)
    earlier = passed_along(product[rows - (taps - 1) :], "ctx", 1)
    extended_narrow = jnp.concatenate([earlier, product], axis=0).reshape(
        rows + taps - 1, groups, per_group
    )
    extended = extended_narrow.astype(jnp.float32)
    forward_band = toeplitz(long_filter[:, ::-1], rows)
    product_wide = product.astype(jnp.float32)
    mixed = jnp.einsum(
        "gts,sgc->tgc",
        forward_band,
        extended,
        precision=lax.Precision.HIGHEST,
        preferred_element_type=jnp.float32,
    ).reshape(rows, channels)
    mixed = mixed + skip_weight[None, :] * product_wide
    stream = residual[0].astype(jnp.float32) + gate_values * mixed
    square_total = lax.psum(jnp.sum(stream * stream, axis=1), "tp")
    inv_rms = lax.rsqrt(square_total / width + 1e-06)
    scaled = stream * inv_rms[:, None]
    normed = (scaled * norm_gain[None, :]).astype(jnp.bfloat16)
    upstream = normed_grad[0].astype(jnp.float32)
    gain_grad = upstream * norm_gain[None, :]
    norm_dot = lax.psum(jnp.sum(gain_grad * scaled, axis=1), "tp")
    stream_grad = inv_rms[:, None] * (gain_grad - scaled * norm_dot[:, None] / width)
    grad_residual = stream_grad.astype(jnp.bfloat16)
    grad_outer = (stream_grad * mixed).astype(jnp.bfloat16)
    gated = (stream_grad * gate_values).astype(jnp.bfloat16)
    later = passed_along(gated[: taps - 1], "ctx", -1)
    ahead = (
        jnp.concatenate([gated, later], axis=0)
        .astype(jnp.float32)
        .reshape(rows + taps - 1, groups, per_group)
    )
    backward_band = toeplitz(long_filter, rows)
    gated_wide = gated.astype(jnp.float32)
    product_grad = jnp.einsum(
        "gts,sgc->tgc",
        backward_band,
        ahead,
        precision=lax.Precision.HIGHEST,
        preferred_element_type=jnp.float32,
    ).reshape(rows, channels)
    product_grad = product_grad + skip_weight[None, :] * gated_wide
    grad_left = (product_grad * value_values).astype(jnp.bfloat16)
    grad_value = (product_grad * left_values).astype(jnp.bfloat16)
    correlation = jnp.einsum(
        "tgc,sgc->gts",
        gated.reshape(rows, groups, per_group),
        extended_narrow,
        preferred_element_type=jnp.float32,
    )
    filter_part = jnp.sum(diagonals(correlation, taps), axis=1)[:, ::-1]
    skip_part = jnp.sum(gated_wide * product_wide, axis=0)
    gain_part = jnp.sum(upstream * scaled, axis=0)
    filter_sum, skip_sum, gain_sum = lax.psum((filter_part, skip_part, gain_part), ("dp", "ctx"))
    devices = lax.axis_size("ctx")
    index = lax.axis_index("ctx")
    per_block = min(devices, max(1, 512 // rows))
    block = rows * per_block
    own_first = index * rows
    query_rows = attn_queries[0].reshape(rows, heads_here, HEAD_DIM)
    attended_wide, log_norm = attend_rows(query_rows, own_first, key_all, value_all, block, scale)
    attended = attended_wide.astype(jnp.bfloat16)
    out_grad = attended_grad[0].reshape(rows, heads_here, HEAD_DIM)
    delta = jnp.sum(out_grad.astype(jnp.float32) * attended.astype(jnp.float32), axis=2).T
    positions = own_first + jnp.arange(rows, dtype=jnp.int32)
    needed = (own_first + rows - 1) // block + 1

    def query_grad_step(number, running_sum):
        keys_here, values_here, allowed = key_block_at(key_all, value_all, number, block, positions)
        scores = jnp.where(allowed[None], scores_block(query_rows, keys_here, scale), -jnp.inf)
        weights = jnp.exp(scores - log_norm[:, :, None]).astype(jnp.bfloat16)
        value_dots = jnp.einsum(
            "rhd,khd->hrk", out_grad, values_here, preferred_element_type=jnp.float32
        )
        score_grad = (weights.astype(jnp.float32) * (value_dots - delta[:, :, None])).astype(
            jnp.bfloat16
        )
        return running_sum + jnp.einsum(
            "hrk,khd->rhd", score_grad, keys_here, preferred_element_type=jnp.float32
        )

    query_grad = lax.fori_loop(
        0, needed, query_grad_step, jnp.zeros((rows, heads_here, HEAD_DIM), jnp.float32)
    )
    grad_queries = (query_grad * scale).astype(jnp.bfloat16)
    stat_norm, stat_delta = (
        lax.all_gather(log_norm.T, "ctx", axis=0, tiled=True),
        lax.all_gather(delta.T, "ctx", axis=0, tiled=True),
    )
    key_own = attn_keys[0].reshape(rows, heads_here, HEAD_DIM)
    value_own = attn_values[0].reshape(rows, heads_here, HEAD_DIM)
    empty = jnp.zeros((rows, heads_here, HEAD_DIM), jnp.float32)
    piece_query = lax.all_gather(attn_queries[0], "ctx", axis=0, tiled=True)
    piece_grad = lax.all_gather(attended_grad[0], "ctx", axis=0, tiled=True)
    count = piece_query.shape[0]
    stride_rows = 512

    def process(number, totals):
        offset = number * stride_rows
        query_part = lax.dynamic_slice_in_dim(piece_query, offset, stride_rows, 0).reshape(
            stride_rows, heads_here, HEAD_DIM
        )
        grad_part = lax.dynamic_slice_in_dim(piece_grad, offset, stride_rows, 0).reshape(
            stride_rows, heads_here, HEAD_DIM
        )
        norm_part = lax.dynamic_slice_in_dim(stat_norm, offset, stride_rows, 0).T
        delta_part = lax.dynamic_slice_in_dim(stat_delta, offset, stride_rows, 0).T
        query_pos = offset + jnp.arange(stride_rows, dtype=jnp.int32)

        def compute(current):
            key_sum, value_sum = current
            allowed = positions[None, :] <= query_pos[:, None]
            scores = jnp.where(allowed[None], scores_block(query_part, key_own, scale), -jnp.inf)
            weights = jnp.exp(scores - norm_part[:, :, None]).astype(jnp.bfloat16)
            value_dots = jnp.einsum(
                "rhd,khd->hrk", grad_part, value_own, preferred_element_type=jnp.float32
            )
            score_grad = (
                weights.astype(jnp.float32) * (value_dots - delta_part[:, :, None])
            ).astype(jnp.bfloat16)
            value_sum = value_sum + jnp.einsum(
                "hrk,rhd->khd", weights, grad_part, preferred_element_type=jnp.float32
            )
            key_sum = key_sum + jnp.einsum(
                "hrk,rhd->khd", score_grad, query_part, preferred_element_type=jnp.float32
            )
            return (key_sum, value_sum)

        def unchanged(current):
            return current

        reaches = offset + stride_rows - 1 >= own_first
        return lax.cond(reaches, compute, unchanged, totals)

    key_sum, value_sum = lax.fori_loop(0, count // stride_rows, process, (empty, empty))
    grad_keys = (key_sum * scale).astype(jnp.bfloat16)
    grad_values = value_sum.astype(jnp.bfloat16)
    flat = (rows, heads_here * HEAD_DIM)
    return (
        normed[None],
        grad_left[None],
        grad_outer[None],
        grad_value[None],
        grad_residual[None],
        filter_sum,
        skip_sum,
        gain_sum,
        attended.reshape(flat)[None],
        grad_queries.reshape(flat)[None],
        grad_keys.reshape(flat)[None],
        grad_values.reshape(flat)[None],
    )


def solution(mesh):
    in_specs = (
        P("dp", "ctx", "tp"),
        P("dp", "ctx", "tp"),
        P("dp", "ctx", "tp"),
        P("dp", "ctx", "tp"),
        P("tp", None),
        P("tp"),
        P("tp"),
        P("dp", "ctx", "tp"),
        P("dp", "ctx", "tp"),
        P("dp", "ctx", "tp"),
        P("dp", "ctx", "tp"),
        P("dp", "ctx", "tp"),
    )
    out_specs = (
        P("dp", "ctx", "tp"),
        P("dp", "ctx", "tp"),
        P("dp", "ctx", "tp"),
        P("dp", "ctx", "tp"),
        P("dp", "ctx", "tp"),
        P("tp", None),
        P("tp"),
        P("tp"),
        P("dp", "ctx", "tp"),
        P("dp", "ctx", "tp"),
        P("dp", "ctx", "tp"),
        P("dp", "ctx", "tp"),
    )
    return jax.shard_map(shards, mesh=mesh, in_specs=in_specs, out_specs=out_specs, check_vma=False)
```

profile of v0, /device:TPU:8, one launch (start us, length us, event | category | flops | bytes accessed | tf_op | source)
XLA Modules:
  0.0 652.6 jit_solution(11089281187697373970)
XLA Ops:
  7.2 1.7 copy.130
  9.0 1.7 copy.129
  10.7 1.7 copy.131
  13.5 3.5 collective-permute-start
  17.0 1.7 copy.137
  19.9 2.4 copy.177
  22.4 2.2 slice.25
  24.6 9.6 %reshape.385 = f32[32,128,255]{2,1,0:T(8,128)} reshape(f32[32,32640]{1,0:T(8,128)} %slice.25) | data formatting | bytes 8355840 | tf_op jit(solution)/shard_map/reshape | solution.py:20
  35.1 2.4 copy.178
  37.5 2.2 slice.27
  39.8 9.5 %reshape.389 = f32[32,128,255]{2,1,0:T(8,128)} reshape(f32[32,32640]{1,0:T(8,128)} %slice.27) | data formatting | bytes 8355840 | tf_op jit(solution)/shard_map/reshape | solution.py:20
  50.0 4.2 fusion.93
  54.5 14.4 %psum.35 = f32[128]{0:T(128)S(1)} all-reduce(f32[128]{0:T(128)S(1)} %get-tuple-element.951), channel_id=1, replica_groups=mesh['dp'=2,'ctx'=32,'tp'=8] {'tp'}, use_global_device_ids=true, to_apply=%region_1.2 | all-reduce | flops 128 | bytes 1024 | tf_op jit(solution)/shard_map/psum | solution.py:129
  69.1 12.6 %psum.36 = f32[128]{0:T(128)S(1)} all-reduce(f32[128]{0:T(128)S(1)} %get-tuple-element.871), channel_id=1, replica_groups=mesh['dp'=2,'ctx'=32,'tp'=8] {'tp'}, use_global_device_ids=true, to_apply=%region_3.4 | all-reduce | flops 128 | bytes 1024 | tf_op jit(solution)/shard_map/psum | solution.py:135
  81.9 3.1 fusion.81
  85.0 5.2 reshape.391
  90.3 2.5 pad.13
  92.7 3.3 copy.179
  96.0 4.8 collective-permute-start.1
  101.8 1.8 slice_reduce_fusion
  103.7 278.5 %all-reduce.3 = (f32[32,128]{1,0:T(8,128)}, f32[512]{0:T(512)}, f32[512]{0:T(512)}) all-reduce(f32[32,128]{1,0:T(8,128)S(1)} %rev.7, f32[512]{0:T(512)S(1)} %get-tuple-element.947, f32[512]{0:T(512)S(1)} %get-tuple-element.870), channel_id=1, replica_groups=mesh['dp'=2,'ctx'=32,'tp'=8] {'dp','ctx'}, use_global_device_ids=true, to_apply=%region_5.6 | all-reduce | flops 5120 | bytes 40960 | tf_op jit(solution)/shard_map/psum | solution.py:167
  382.3 4.2 fusion.94
  387.5 6.4 copy.135
  393.9 1.7 while.56
  394.1 1.4 fusion.125
  395.7 2.0 while.57
  395.9 1.8 fusion.129
  398.0 3.4 while.58
  398.2 1.4 fusion.135
  399.6 1.8 fusion.136
  402.4 140.3 %all_gather.21 = f32[4096,4]{1,0:T(8,128)S(1)} all-gather(f32[128,4]{1,0:T(8,128)S(1)} %copy.167), channel_id=1, replica_groups=mesh['dp'=2,'ctx'=32,'tp'=8] {'ctx'}, dimensions={0}, use_global_device_ids=true | all-gather | bytes 67584 | tf_op jit(solution)/shard_map/all_gather | solution.py:201
  543.4 74.2 %all_gather.20 = f32[4096,4]{0,1:T(4,128)S(1)} all-gather(f32[128,4]{0,1:T(4,128)S(1)} %bitcast.213), channel_id=1, replica_groups=mesh['dp'=2,'ctx'=32,'tp'=8] {'ctx'}, dimensions={0}, use_global_device_ids=true | all-gather | bytes 67584 | tf_op jit(solution)/shard_map/all_gather | solution.py:200
  617.7 25.9 %while.59 = (s32[]{:T(128)}, f32[128,4,128]{2,0,1:T(8,128)S(1)}, f32[128,4,128]{2,0,1:T(8,128)S(1)}, s32[]{:T(128)}, f32[4096,4]{0,1:T(4,128)S(1)}, /*index=5*/f...) while((s32[]{:T(128)}, f32[128,4,128]{2,0,1:T(8,128)S(1)}, ...), condition=%wide.region_22.23_spmd.clone.clone, body=%wide.region_19.22_spmd.clone.clone.sunk | while | flops 270729856 | bytes 7268725 | solution.py:248
  617.7 3.2 conditional.4
  617.8 1.3 constant_dynamic-slice_fusion
  621.0 3.2 conditional.4
  621.0 1.3 constant_dynamic-slice_fusion
  624.2 3.2 conditional.4
  624.2 1.3 constant_dynamic-slice_fusion
  627.5 3.2 conditional.4
  627.5 1.3 constant_dynamic-slice_fusion
  630.7 3.2 conditional.4
  630.7 1.3 constant_dynamic-slice_fusion
  633.9 3.2 conditional.4
  633.9 1.3 constant_dynamic-slice_fusion
  637.2 3.2 conditional.4
  637.2 1.3 constant_dynamic-slice_fusion
  640.4 3.2 conditional.4
  (177 shorter events, 27.8 us)
Async XLA Ops:
  7.2 380.3 %all-gather.11.cloned.1.call-start = ((), (), s32[]{:S(2)}) async-start(), calls=%async_computation.1 | async-start | bytes 4325376 | tf_op jit(solution)/shard_map/all_gather | solution.py:103
  8.9 386.8 %all-gather.9.cloned.1.call-start = ((), (), s32[]{:S(2)}) async-start(), calls=%async_computation | async-start | bytes 4325376 | tf_op jit(solution)/shard_map/all_gather | solution.py:104
  10.7 607.0 %all-gather.13.cloned.1.call-start = ((), (), s32[]{:S(2)}) async-start(), calls=%async_computation.2 | async-start | bytes 4325376 | tf_op jit(solution)/shard_map/all_gather | solution.py:206
  12.4 605.2 %all-gather.15.cloned.1.call-start = ((), (), s32[]{:S(2)}) async-start(), calls=%async_computation.3 | async-start | bytes 4325376 | tf_op jit(solution)/shard_map/all_gather | solution.py:207
  13.5 36.3 %collective-permute-start = (bf16[127,512]{1,0:T(8,128)(2,1)S(1)}, bf16[127,512]{1,0:T(8,128)(2,1)S(1)}, u32[]{:S(2)}, u32[]{:S(2)}) collective-permute-start(bf16[127,512]{1,0:T(8,128)(2,1)S(1)} %slice_bitcast_fusion), channel_id=1, source_target_pairs={{0,8},{8,16},{16,24},{24,32},{32,40},{40,48},{48,56},{56,64},{64,7... | collective-permute-start | bytes 390152 | tf_op jit(solution)/shard_map/ppermute | solution.py:12
  24.5 9.7 %copy-start.1 = (bf16[1,128,512]{2,1,0:T(8,128)(2,1)S(1)}, bf16[1,128,512]{2,1,0:T(8,128)(2,1)}, u32[]{:S(2)}) copy-start(bf16[1,128,512]{2,1,0:T(8,128)(2,1)} %param.29) | copy-start | bytes 393220
  24.5 9.8 %copy-start.3 = (bf16[1,128,512]{2,1,0:T(8,128)(2,1)S(1)}, bf16[1,128,512]{2,1,0:T(8,128)(2,1)}, u32[]{:S(2)}) copy-start(bf16[1,128,512]{2,1,0:T(8,128)(2,1)} %param.25) | copy-start | bytes 393220
  24.5 9.9 %copy-start = (bf16[1,128,512]{2,1,0:T(8,128)(2,1)S(1)}, bf16[1,128,512]{2,1,0:T(8,128)(2,1)}, u32[]{:S(2)}) copy-start(bf16[1,128,512]{2,1,0:T(8,128)(2,1)} %param.23) | copy-start | bytes 393220
  24.6 10.0 %copy-start.10 = (f32[512]{0:T(512)S(1)}, f32[512]{0:T(512)}, u32[]{:S(2)}) copy-start(f32[512]{0:T(512)} %param.28) | copy-start | bytes 6148
  24.6 10.1 %copy-start.11 = (f32[512]{0:T(512)S(1)}, f32[512]{0:T(512)}, u32[]{:S(2)}) copy-start(f32[512]{0:T(512)} %param.27) | copy-start | bytes 6148
  24.6 10.2 %copy-start.9 = (f32[32,128]{1,0:T(8,128)S(1)}, f32[32,128]{1,0:T(8,128)}, u32[]{:S(2)}) copy-start(f32[32,128]{1,0:T(8,128)} %param.26) | copy-start | bytes 49156
  39.7 9.5 %copy-start.4 = (bf16[1,128,512]{1,2,0:T(8,128)(2,1)S(1)}, bf16[1,128,512]{1,2,0:T(8,128)(2,1)}, u32[]{:S(2)}) copy-start(bf16[1,128,512]{1,2,0:T(8,128)(2,1)} %copy.131) | copy-start | bytes 393220
  39.7 9.6 %copy-start.2 = (bf16[1,128,512]{1,2,0:T(8,128)(2,1)S(1)}, bf16[1,128,512]{1,2,0:T(8,128)(2,1)}, u32[]{:S(2)}) copy-start(bf16[1,128,512]{1,2,0:T(8,128)(2,1)} %copy.137) | copy-start | bytes 393220
  39.7 9.7 %copy-start.6 = (bf16[1,128,512]{1,2,0:T(8,128)(2,1)S(1)}, bf16[1,128,512]{1,2,0:T(8,128)(2,1)}, u32[]{:S(2)}) copy-start(bf16[1,128,512]{1,2,0:T(8,128)(2,1)} %copy.130) | copy-start | bytes 393220
  39.7 9.9 %copy-start.5 = (bf16[1,128,512]{1,2,0:T(8,128)(2,1)S(1)}, bf16[1,128,512]{1,2,0:T(8,128)(2,1)}, u32[]{:S(2)}) copy-start(bf16[1,128,512]{1,2,0:T(8,128)(2,1)} %copy.129) | copy-start | bytes 393220
  96.0 286.1 %collective-permute-start.1 = (bf16[127,512]{1,0:T(8,128)(2,1)S(1)}, bf16[127,512]{1,0:T(8,128)(2,1)S(1)}, u32[]{:S(2)}, u32[]{:S(2)}) collective-permute-start(bf16[127,512]{1,0:T(8,128)(2,1)S(1)} %bitcast.212), channel_id=1, source_target_pairs={{8,0},{16,8},{24,16},{32,24},{40,32},{48,40},{56,48},{64,56},{72,6... | collective-permute-start | bytes 390152 | tf_op jit(solution)/shard_map/ppermute | solution.py:12
  101.8 284.8 %copy-start.7 = (bf16[1,128,512]{2,1,0:T(8,128)(2,1)S(1)}, bf16[1,128,512]{2,1,0:T(8,128)(2,1)}, u32[]{:S(2)}) copy-start(bf16[1,128,512]{2,1,0:T(8,128)(2,1)} %param.24) | copy-start | bytes 393220
  101.8 284.8 %copy-start.8 = (bf16[1,128,512]{2,1,0:T(8,128)(2,1)S(1)}, bf16[1,128,512]{2,1,0:T(8,128)(2,1)}, u32[]{:S(2)}) copy-start(bf16[1,128,512]{2,1,0:T(8,128)(2,1)} %param.22) | copy-start | bytes 393220
Sparse Core Ops, SparseCore 0:
  10.6 144.1 all-gather.10
  157.4 139.1 all-gather.8
  299.2 141.8 all-gather.12
  443.5 144.5 all-gather.14
where the time goes:
time: 654 us; the launch traced here: 653 us
  blocking collectives  520 us (80%)
  local copies, waits for them, and re-layouts  70.3 us (11%)
  matrix products  31.3 us (5%)
  between operations  14.2 us (2%)
  starting transfers between devices  8.48 us (1%)
  other arithmetic  6.97 us (1%)
    psum x1, blocking collectives, shards(): lax.psum((filter_part, skip_part, gain_part), ('dp', 'ctx'))  278 us
    all_gather x1, blocking collectives, shards(): lax.all_gather(delta.T, 'ctx', axis=0, tiled=True)  140 us
    all_gather x1, blocking collectives, shards(): lax.all_gather(log_norm.T, 'ctx', axis=0, tiled=True)  74.2 us
    unnamed x40, local copies, waits for them, and re-layouts  23.3 us
    reshape x2, local copies, waits for them, and re-layouts, toeplitz(): return tiled.reshape(groups, rows, width)  19.1 us
    psum x1, blocking collectives, shards(): square_total = lax.psum(jnp.sum(stream * stream, axis=1), 'tp')  14.4 us
  transfers between devices with their start and end apart: 6, of which 0 were waited for; matrix products, arithmetic and copies ran while one was open for 12% of the time, Pallas kernels for 0%

commit v1 on v0

v1 whole, which is shorter than its diff:
```python
import math

import jax
import jax.numpy as jnp
from jax import lax
from jax.experimental import pallas as pl
from jax.experimental.pallas import tpu as pltpu
from jax.sharding import PartitionSpec as P

HEAD_DIM = 128
LANES = 128
LOG2E = math.log2(math.e)
F32 = jnp.float32
BF16 = jnp.bfloat16
VMEM = pltpu.VMEM


def passed_along(value, axis, steps):
    count = lax.axis_size(axis)
    initial, last = (max(0, -steps), min(count, count - steps))
    return lax.ppermute(value, axis, [(source, source + steps) for source in range(initial, last)])


def dot_nt(a, b):
    return lax.dot_general(a, b, (((1,), (1,)), ((), ())), preferred_element_type=F32)


def dot_nn(a, b):
    return lax.dot_general(a, b, (((1,), (0,)), ((), ())), preferred_element_type=F32)


def whole(count):
    return [pl.BlockSpec(memory_space=VMEM) for _ in range(count)]


def row_of(column):
    return jnp.transpose(jnp.broadcast_to(column, (column.shape[0], LANES)))[0:1]


def query_kernel(place_ref, own_ref, kv_ref, att_ref, dq_ref, stat_ref, s_ref, p_ref):
    place = place_ref[0]
    ring, strips, _, rows, depth = kv_ref.shape
    span = ring * rows
    factor = HEAD_DIM ** (-0.5) * LOG2E
    line = lax.broadcasted_iota(jnp.int32, (rows, span), 0) + place * rows
    allowed = lax.broadcasted_iota(jnp.int32, (rows, span), 1) <= line
    tops = [None] * strips
    for zk in range(strips):
        key = kv_ref[:, zk, 0].reshape(span, depth)
        query = own_ref[zk:, 0].reshape((strips - zk) * rows, depth)
        scores = dot_nt(query, key) * factor
        for zq in range(zk, strips):
            part = scores[(zq - zk) * rows : (zq - zk + 1) * rows]
            if zq == zk:
                part = jnp.where(allowed, part, -1e30)
            s_ref[zq * rows : (zq + 1) * rows, zk * span : (zk + 1) * span] = part
            top = jnp.max(part, axis=1, keepdims=True)
            tops[zq] = top if zk == 0 else jnp.maximum(tops[zq], top)
    totals = [jnp.zeros((rows, 1), F32) for _ in range(strips)]
    outs = [jnp.zeros((rows, depth), F32) for _ in range(strips)]
    for zk in range(strips):
        columns = slice(zk * span, (zk + 1) * span)
        for zq in range(zk, strips):
            lines = slice(zq * rows, (zq + 1) * rows)
            power = jnp.exp2(s_ref[lines, columns] - tops[zq])
            totals[zq] = totals[zq] + jnp.sum(power, axis=1, keepdims=True)
            p_ref[lines, columns] = power.astype(BF16)
        value = kv_ref[:, zk, 1].reshape(span, depth)
        added = dot_nn(p_ref[zk * rows :, columns], value)
        for zq in range(zk, strips):
            outs[zq] = outs[zq] + added[(zq - zk) * rows : (zq - zk + 1) * rows]
    inverses, deltas = ([], [])
    for zq in range(strips):
        inverse = 1.0 / totals[zq]
        attended = (outs[zq] * inverse).astype(BF16)
        att_ref[zq] = attended
        delta = jnp.sum(
            own_ref[zq, 1].astype(F32) * attended.astype(F32), axis=1, keepdims=True
        )
        stat_ref[zq, 0:1] = row_of(tops[zq] + jnp.log(totals[zq]) * LOG2E)
        stat_ref[zq, 1:2] = row_of(delta)
        inverses.append(inverse)
        deltas.append(delta)
    grads = [jnp.zeros((rows, depth), F32) for _ in range(strips)]
    for zk in range(strips):
        columns = slice(zk * span, (zk + 1) * span)
        key = kv_ref[:, zk, 0].reshape(span, depth)
        value = kv_ref[:, zk, 1].reshape(span, depth)
        out_grad = own_ref[zk:, 1].reshape((strips - zk) * rows, depth)
        dots = dot_nt(out_grad, value)
        parts = []
        for zq in range(zk, strips):
            lines = slice(zq * rows, (zq + 1) * rows)
            here = dots[(zq - zk) * rows : (zq - zk + 1) * rows]
            parts.append((p_ref[lines, columns].astype(F32) * (here - deltas[zq])).astype(BF16))
        added = dot_nn(jnp.concatenate(parts, axis=0), key)
        for zq in range(zk, strips):
            grads[zq] = grads[zq] + added[(zq - zk) * rows : (zq - zk + 1) * rows]
    for zq in range(strips):
        dq_ref[zq] = (grads[zq] * (inverses[zq] * HEAD_DIM ** (-0.5))).astype(BF16)


def key_kernel(place_ref, own_ref, qd_ref, stat_ref, dk_ref, dv_ref):
    place = place_ref[0]
    ring, strips, _, rows, depth = qd_ref.shape
    span = ring * rows
    factor = HEAD_DIM ** (-0.5) * LOG2E
    line = lax.broadcasted_iota(jnp.int32, (rows, span), 0) + place * rows
    allowed = lax.broadcasted_iota(jnp.int32, (rows, span), 1) >= line
    key_sums = [jnp.zeros((rows, depth), F32) for _ in range(strips)]
    value_sums = [jnp.zeros((rows, depth), F32) for _ in range(strips)]
    for zq in range(strips):
        count = zq + 1
        query = qd_ref[:, zq, 0].reshape(span, depth)
        out_grad = qd_ref[:, zq, 1].reshape(span, depth)
        norm = jnp.concatenate([stat_ref[r, zq, 0:1] for r in range(ring)], axis=1)
        delta = jnp.concatenate([stat_ref[r, zq, 1:2] for r in range(ring)], axis=1)
        key = own_ref[:count, 0].reshape(count * rows, depth)
        value = own_ref[:count, 1].reshape(count * rows, depth)
        scores = dot_nt(key, query) * factor - norm
        last = jnp.where(allowed, scores[zq * rows :], -1e30)
        if zq:
            scores = jnp.concatenate([scores[: zq * rows], last], axis=0)
        else:
            scores = last
        weights = jnp.exp2(scores).astype(BF16)
        dots = dot_nt(value, out_grad)
        score_grad = (weights.astype(F32) * (dots - delta)).astype(BF16)
        value_added = dot_nn(weights, out_grad)
        key_added = dot_nn(score_grad, query)
        for zk in range(count):
            lines = slice(zk * rows, (zk + 1) * rows)
            value_sums[zk] = value_sums[zk] + value_added[lines]
            key_sums[zk] = key_sums[zk] + key_added[lines]
    for zk in range(strips):
        dk_ref[zk] = (key_sums[zk] * HEAD_DIM ** (-0.5)).astype(BF16)
        dv_ref[zk] = value_sums[zk].astype(BF16)


def fill_phases(first, second, ext_ref, phase_ref):
    rows = first.shape[0]
    ext_ref[:rows] = first
    ext_ref[rows:] = second
    for r in range(8):
        phase_ref[r] = ext_ref[r : r + 2 * rows - 8]


def mix_kernel(
    left_ref, value_ref, before_ref, gate_ref, residual_ref, upstream_ref, taps_ref, skip_ref,
    gain_ref, mixed_ref, stream_ref, sums_ref, ext_ref, phase_ref,
):
    rows = left_ref.shape[0]
    taps = taps_ref.shape[0]
    product = (left_ref[...].astype(F32) * value_ref[...].astype(F32)).astype(BF16).astype(F32)
    fill_phases(before_ref[...].astype(F32), product, ext_ref, phase_ref)
    mixed = (taps_ref[0:1] + skip_ref[...]) * product
    for tap in range(1, taps):
        a, r = divmod(rows - tap, 8)
        mixed = mixed + taps_ref[tap : tap + 1] * phase_ref[r, 8 * a : 8 * a + rows]
    stream = residual_ref[...].astype(F32) + gate_ref[...].astype(F32) * mixed
    mixed_ref[...] = mixed
    stream_ref[...] = stream
    upstream = upstream_ref[...].astype(F32) * gain_ref[...]

    @pl.when(pl.program_id(0) == 0)
    def _():
        sums_ref[...] = jnp.zeros_like(sums_ref)

    sums_ref[0] += stream * stream
    sums_ref[1] += upstream * stream


def norm_kernel(
    upstream_ref, gate_ref, mixed_ref, stream_ref, gain_ref, totals_ref,
    normed_ref, residual_grad_ref, outer_grad_ref, gated_ref, gain_grad_ref, *, width,
):
    inv_rms = lax.rsqrt(totals_ref[:, 0:1] * (1.0 / width) + 1e-06)
    norm_dot = totals_ref[:, 1:2] * inv_rms * (1.0 / width)
    gain = gain_ref[...]
    upstream = upstream_ref[...].astype(F32)
    scaled = stream_ref[...] * inv_rms
    normed_ref[...] = (scaled * gain).astype(BF16)
    gain_grad_ref[...] = jnp.sum(upstream * scaled, axis=0, keepdims=True)
    stream_grad = inv_rms * (upstream * gain - scaled * norm_dot)
    residual_grad_ref[...] = stream_grad.astype(BF16)
    outer_grad_ref[...] = (stream_grad * mixed_ref[...]).astype(BF16)
    gated_ref[...] = (stream_grad * gate_ref[...].astype(F32)).astype(BF16)


def back_kernel(
    left_ref, value_ref, before_ref, gated_ref, after_ref, taps_ref, skip_ref,
    left_grad_ref, value_grad_ref, filter_ref, skip_grad_ref, ext_ref, phase_ref,
):
    rows = left_ref.shape[0]
    taps = taps_ref.shape[0]
    left = left_ref[...].astype(F32)
    value = value_ref[...].astype(F32)
    product = (left * value).astype(BF16).astype(F32)
    gated = gated_ref[...].astype(F32)
    fill_phases(gated, after_ref[...].astype(F32), ext_ref, phase_ref)
    grad = (skip_ref[...] + taps_ref[0:1]) * gated
    for tap in range(1, taps):
        a, r = divmod(tap, 8)
        grad = grad + taps_ref[tap : tap + 1] * phase_ref[r, 8 * a : 8 * a + rows]
    left_grad_ref[...] = (grad * value).astype(BF16)
    value_grad_ref[...] = (grad * left).astype(BF16)
    fill_phases(before_ref[...].astype(F32), product, ext_ref, phase_ref)
    direct = jnp.sum(gated * product, axis=0, keepdims=True)
    skip_grad_ref[...] = direct
    filter_ref[0:1] = direct
    for tap in range(1, taps):
        a, r = divmod(rows - tap, 8)
        filter_ref[tap : tap + 1] = jnp.sum(
            gated * phase_ref[r, 8 * a : 8 * a + rows], axis=0, keepdims=True
        )


def shape_of(shape, dtype):
    return jax.ShapeDtypeStruct(shape, dtype)


def shards(
    left_stream,
    outer_gate,
    value_stream,
    residual,
    long_filter,
    skip_weight,
    norm_gain,
    normed_grad,
    attn_queries,
    attn_keys,
    attn_values,
    attended_grad,
):
    rows = left_stream.shape[1]
    channels = left_stream.shape[2]
    groups, taps = long_filter.shape
    per_group = channels // groups
    width = channels * lax.axis_size("tp")
    heads = attn_queries.shape[2] // HEAD_DIM
    devices = lax.axis_size("ctx")
    ring = devices // heads
    index = lax.axis_index("ctx")
    place = (index % ring).astype(jnp.int32).reshape(1)
    across = [[strip * ring + spot for strip in range(heads)] for spot in range(ring)]
    along = [[strip * ring + spot for spot in range(ring)] for strip in range(heads)]

    stacked = jnp.stack([attn_keys[0], attn_values[0], attn_queries[0], attended_grad[0]])
    stacked = stacked.reshape(4, rows, heads, HEAD_DIM).transpose(2, 0, 1, 3)
    own = lax.all_to_all(stacked, "ctx", 0, 0, axis_index_groups=across, tiled=True)
    own_kv, own_qd = (own[:, :2], own[:, 2:])
    all_kv = lax.all_gather(own_kv, "ctx", axis=0, axis_index_groups=along, tiled=False)
    all_qd = lax.all_gather(own_qd, "ctx", axis=0, axis_index_groups=along, tiled=False)

    left, value, gate = (left_stream[0], value_stream[0], outer_gate[0])
    upstream = normed_grad[0]
    product = (left.astype(F32) * value.astype(F32)).astype(BF16)
    before = passed_along(product, "ctx", 1)
    taps_rows = jnp.repeat(long_filter.T, per_group, axis=1)
    skip, gain = (skip_weight[None, :], norm_gain[None, :])
    grid = (channels // LANES,)
    block = pl.BlockSpec((rows, LANES), lambda j: (0, j))
    tap_block = pl.BlockSpec((taps, LANES), lambda j: (0, j))
    line = pl.BlockSpec((1, LANES), lambda j: (0, j))
    phases = [VMEM((2 * rows, LANES), F32), VMEM((8, 2 * rows - 8, LANES), F32)]
    size = rows * channels
    mixed, stream, sums = pl.pallas_call(
        mix_kernel,
        grid=grid,
        in_specs=[block] * 6 + [tap_block, line, line],
        out_specs=[block, block, pl.BlockSpec((2, rows, LANES), lambda j: (0, 0, 0))],
        out_shape=[
            shape_of((rows, channels), F32),
            shape_of((rows, channels), F32),
            shape_of((2, rows, LANES), F32),
        ],
        scratch_shapes=phases,
        cost_estimate=pl.CostEstimate(
            flops=2 * taps * size, bytes_accessed=20 * size, transcendentals=0
        ),
        name="mix",
    )(left, value, before, gate, residual[0], upstream, taps_rows, skip, gain)
    totals = lax.psum(jnp.sum(sums, axis=2), "tp").T
    normed, grad_residual, grad_outer, gated, gain_part = pl.pallas_call(
        lambda *refs: norm_kernel(*refs, width=width),
        in_specs=whole(6),
        out_specs=whole(5),
        out_shape=[shape_of((rows, channels), BF16)] * 4 + [shape_of((1, channels), F32)],
        cost_estimate=pl.CostEstimate(
            flops=20 * size, bytes_accessed=20 * size, transcendentals=0
        ),
        name="norm",
    )(upstream, gate, mixed, stream, gain, totals)
    after = passed_along(gated, "ctx", -1)
    grad_left, grad_value, filter_rows, skip_part = pl.pallas_call(
        back_kernel,
        grid=grid,
        in_specs=[block] * 5 + [tap_block, line],
        out_specs=[block, block, tap_block, line],
        out_shape=[
            shape_of((rows, channels), BF16),
            shape_of((rows, channels), BF16),
            shape_of((taps, channels), F32),
            shape_of((1, channels), F32),
        ],
        scratch_shapes=phases,
        cost_estimate=pl.CostEstimate(
            flops=4 * taps * size, bytes_accessed=20 * size, transcendentals=0
        ),
        name="back",
    )(left, value, before, gated, after, taps_rows, skip)
    member = (
        jnp.arange(channels, dtype=jnp.int32)[None, :] // per_group
        == jnp.arange(groups, dtype=jnp.int32)[:, None]
    ).astype(F32)
    filter_part = lax.dot_general(
        member, filter_rows, (((1,), (1,)), ((), ())), precision=lax.Precision.HIGHEST
    )
    small = jnp.concatenate(
        [filter_part.reshape(-1), skip_part.reshape(-1), gain_part.reshape(-1)]
    )
    small = lax.psum(small, ("dp", "ctx"))
    cut = groups * taps
    filter_sum = small[:cut].reshape(groups, taps)
    skip_sum, gain_sum = (small[cut : cut + channels], small[cut + channels :])

    smem = pl.BlockSpec(memory_space=pltpu.SMEM)
    blocks = (heads, rows, HEAD_DIM)
    pairs = heads * (heads + 1) // 2 * rows * ring * rows
    attended, grad_queries, stats = pl.pallas_call(
        query_kernel,
        in_specs=[smem] + whole(2),
        out_specs=whole(3),
        out_shape=[shape_of(blocks, BF16), shape_of(blocks, BF16), shape_of((heads, 2, rows), F32)],
        scratch_shapes=[
            VMEM((heads * rows, devices * rows), F32),
            VMEM((heads * rows, devices * rows), BF16),
        ],
        cost_estimate=pl.CostEstimate(
            flops=8 * HEAD_DIM * pairs, bytes_accessed=3 << 20, transcendentals=pairs
        ),
        name="query",
    )(place, own_qd, all_kv)
    all_stats = lax.all_gather(stats, "ctx", axis=0, axis_index_groups=along, tiled=False)
    grad_keys, grad_values = pl.pallas_call(
        key_kernel,
        in_specs=[smem] + whole(3),
        out_specs=whole(2),
        out_shape=[shape_of(blocks, BF16)] * 2,
        cost_estimate=pl.CostEstimate(
            flops=8 * HEAD_DIM * pairs, bytes_accessed=3 << 20, transcendentals=pairs
        ),
        name="key",
    )(place, own_kv, all_qd, all_stats)
    back = jnp.stack([attended, grad_queries, grad_keys, grad_values], axis=1)
    back = lax.all_to_all(back, "ctx", 0, 0, axis_index_groups=across, tiled=True)
    back = back.transpose(1, 2, 0, 3).reshape(4, rows, heads * HEAD_DIM)
    return (
        normed[None],
        grad_left[None],
        grad_outer[None],
        grad_value[None],
        grad_residual[None],
        filter_sum,
        skip_sum,
        gain_sum,
        back[0:1],
        back[1:2],
        back[2:3],
        back[3:4],
    )


def solution(mesh):
    in_specs = (
        P("dp", "ctx", "tp"),
        P("dp", "ctx", "tp"),
        P("dp", "ctx", "tp"),
        P("dp", "ctx", "tp"),
        P("tp", None),
        P("tp"),
        P("tp"),
        P("dp", "ctx", "tp"),
        P("dp", "ctx", "tp"),
        P("dp", "ctx", "tp"),
        P("dp", "ctx", "tp"),
        P("dp", "ctx", "tp"),
    )
    out_specs = (
        P("dp", "ctx", "tp"),
        P("dp", "ctx", "tp"),
        P("dp", "ctx", "tp"),
        P("dp", "ctx", "tp"),
        P("dp", "ctx", "tp"),
        P("tp", None),
        P("tp"),
        P("tp"),
        P("dp", "ctx", "tp"),
        P("dp", "ctx", "tp"),
        P("dp", "ctx", "tp"),
        P("dp", "ctx", "tp"),
    )
    return jax.shard_map(shards, mesh=mesh, in_specs=in_specs, out_specs=out_specs, check_vma=False)
```

time: 654 us -> 438 us (0.67)
  the two profiles are of different devices: /device:TPU:8 before, /device:TPU:2 now
where the time goes in v1:
time: 438 us; the launch traced here: 437 us
  blocking collectives  351 us (80%)
  Pallas kernels  24.7 us (6%)
  waiting for transfers between devices  20.5 us (5%)
  between operations  14.2 us (3%)
  local copies, waits for them, and re-layouts  13 us (3%)
  starting transfers between devices  10.1 us (2%)
    psum x1, blocking collectives, shards(): small = lax.psum(small, ('dp', 'ctx'))  281 us
    all_gather x1, blocking collectives, shards(): lax.all_gather(stats, 'ctx', axis=0, axis_index_groups=along, tiled=False)  26.1 us
    psum x1, blocking collectives, shards(): totals = lax.psum(jnp.sum(sums, axis=2), 'tp').T  22.1 us
    all_to_all x1, blocking collectives, shards(): lax.all_to_all(stacked, 'ctx', 0, 0, axis_index_groups=across, tiled=True)  21.5 us
    all_gather x1, waiting for transfers between devices, shards(): lax.all_gather(own_qd, 'ctx', axis=0, axis_index_groups=along, tiled=False)  10.7 us
  transfers between devices with their start and end apart: 5, of which 3 were waited for; matrix products, arithmetic and copies ran while one was open for 2% of the time, Pallas kernels for 6%

profile of v1, /device:TPU:2, one launch (start us, length us, event | category | flops | bytes accessed | tf_op | source)
XLA Modules:
  0.0 437.1 jit_solution(560531150117754450)
XLA Ops:
  7.2 0.0 all-gather.6.cloned.1.call-start
  7.2 1.0 copy.43
  8.3 1.0 copy.44
  9.3 1.0 copy.45
  10.3 1.0 copy.46
  11.3 0.1 pad_maximum_fusion
  11.4 0.0 copy-start
  11.4 0.0 copy-start.1
  11.4 0.0 copy-start.6
  11.5 0.3 copy.47
  11.7 21.5 %all_to_all.10 = bf16[4,4,128,128]{3,2,1,0:T(8,128)(2,1)S(1)} all-to-all(bf16[4,4,128,128]{3,2,1,0:T(8,128)(2,1)S(1)} %bitcast.41), channel_id=1, replica_groups={{0,64,128,192},{8,72,136,200},{16,80,144,208},{24,88,152,216},{32,96,16..., dimensions={0} | all-to-all | bytes 1048576 | tf_op jit(solution)/shard_map/all_to_all | solution.py:251
  33.3 0.8 fusion.5
  34.1 0.0 all-gather.6.cloned.1.call-update
  34.2 0.0 all-gather.8.cloned.1.call-start
  34.2 0.7 all-gather.8.cloned.1.call-update
  35.0 3.5 collective-permute-start
  38.5 0.8 copy.40.taps_ref
  39.4 1.6 collective-permute-done.before_ref
  41.0 0.7 copy-done.2
  41.6 4.6 %mix.1 = (f32[128,512]{1,0:T(8,128)}, f32[128,512]{1,0:T(8,128)}, f32[2,128,128]{2,1,0:T(8,128)}) custom-call(bf16[128,512]{1,0:T(8,128)(2,1)} %bitcast.42, bf16[128,512]{1,0:T(8,128)(2,1)} %bitcast.44, bf16[128,512]{1,0:T(8,128)(2,1)} %copy-done.2, bf16[128,512]{1,0:T(8,128)(2,1)} %bitcast.53, bf16[128,512]{1,0:T(8,128)(2,1)} %bitcast.56, ...), custom_call_target="tpu_custom_call" | custom-call | flops 16777216 | bytes 1310720 | tf_op jit(solution)/shard_map/mix/pallas_call | solution.py:268
  46.2 1.0 reduce_sum.9
  47.2 0.1 copy.41
  47.4 22.1 %psum.14.refs_5_ = f32[128,2]{1,0:T(8,128)} all-reduce(f32[128,2]{1,0:T(8,128)S(1)} %bitcast.55), channel_id=1, replica_groups=mesh['dp'=2,'ctx'=32,'tp'=8] {'tp'}, use_global_device_ids=true, to_apply=%region_1.2 | all-reduce | flops 256 | bytes 2048 | tf_op jit(solution)/shard_map/psum | solution.py:284
  69.5 2.1 norm.1
  71.6 1.3 collective-permute-start.1
  72.9 7.4 %all-gather.6.cloned.1.call-done = bf16[32,2,128,128]{3,2,1,0:T(8,128)(2,1)} async-done(((bf16[4,2,128,128]{3,2,1,0:T(8,128)(2,1)}), bf16[32,2,128,128]{3,2,1,0:T(8,128)(2,1)}) %all-gather.6.cloned.1.call-update) | async-done | bytes 2097168 | tf_op jit(solution)/shard_map/all_gather | solution.py:253
  80.3 6.1 %query.1 = (bf16[4,128,128]{2,1,0:T(8,128)(2,1)}, bf16[4,128,128]{2,1,0:T(8,128)(2,1)}, f32[4,2,128]{2,1,0:T(2,128)}) custom-call(s32[1]{0:T(128)} %bitcast.19.place_ref, bf16[4,2,128,128]{3,2,1,0:T(8,128)(2,1)} %get-tuple-element.74.own_ref, bf16[8,4,2,128,128]{4,3,2,1,0:T(8,128)(2,1)} %bitcast.69), custom_call_target="tpu_custom_call" | custom-call | flops 1342177280 | bytes 3145728 | tf_op jit(solution)/shard_map/query/pallas_call | solution.py:331
  86.4 26.1 %all-gather.2 = f32[32,2,128]{2,1,0:T(2,128)} all-gather(f32[4,2,128]{2,1,0:T(2,128)} %get-tuple-element.43), channel_id=4, replica_groups={{0,8,16,24,32,40,48,56},{64,72,80,88,96,104,112,120},{128,136,144,152,1..., dimensions={0}, use_global_device_ids=true | all-gather | bytes 36864 | tf_op jit(solution)/shard_map/all_gather | solution.py:345
  112.5 10.7 %all-gather.8.cloned.1.call-done = bf16[32,2,128,128]{3,2,1,0:T(8,128)(2,1)} async-done(((bf16[4,2,128,128]{3,2,1,0:T(8,128)(2,1)}), bf16[32,2,128,128]{3,2,1,0:T(8,128)(2,1)}) %all-gather.8.cloned.1.call-update) | async-done | bytes 2097168 | tf_op jit(solution)/shard_map/all_gather | solution.py:254
  123.2 5.4 %key.1 = (bf16[4,128,128]{2,1,0:T(8,128)(2,1)}, bf16[4,128,128]{2,1,0:T(8,128)(2,1)}) custom-call(s32[1]{0:T(128)} %bitcast.19.place_ref, bf16[4,2,128,128]{3,2,1,0:T(8,128)(2,1)} %get-tuple-element.75.own_ref, bf16[8,4,2,128,128]{4,3,2,1,0:T(8,128)(2,1)} %bitcast.70, f32[8,4,2,128]{3,2,1,0:T(2,128)} %bitcast.61), custom_call_target="tpu_custom_call" | custom-call | flops 1342177280 | bytes 3145728 | tf_op jit(solution)/shard_map/key/pallas_call | solution.py:346
  128.7 1.0 pad_maximum_fusion.1
  129.7 0.8 copy.48
  130.5 5.3 %all-to-all-start.1 = ((bf16[4,4,128,128]{3,2,1,0:T(8,128)(2,1)}), bf16[4,4,128,128]{3,2,1,0:T(8,128)(2,1)S(1)}, u32[]{:S(2)}, u32[]{:S(2)}) async-start(bf16[4,4,128,128]{3,2,1,0:T(8,128)(2,1)} %copy.48), calls=%async_computation.1 | async-start | bytes 1048576 | tf_op jit(solution)/shard_map/all_to_all | solution.py:357
  135.8 0.0 collective-permute-done.1.after_ref
  135.8 0.0 copy-start.3
  135.8 0.6 copy-done.3
  136.5 6.5 %back.1 = (bf16[128,512]{1,0:T(8,128)(2,1)}, bf16[128,512]{1,0:T(8,128)(2,1)}, f32[128,512]{1,0:T(8,128)}, f32[1,512]{1,0:T(1,128)}) custom-call(bf16[128,512]{1,0:T(8,128)(2,1)} %bitcast.43, bf16[128,512]{1,0:T(8,128)(2,1)} %bitcast.45, bf16[128,512]{1,0:T(8,128)(2,1)} %copy-done.2, bf16[128,512]{1,0:T(8,128)(2,1)} %get-tuple-element.33.gated_ref, ...), custom_call_target="tpu_custom_call" | custom-call | flops 33554432 | bytes 1310720 | tf_op jit(solution)/shard_map/back/pallas_call | solution.py:296
  143.0 1.2 convolution_bitcast_fusion
  144.2 0.7 pad_maximum_fusion.2
  144.9 280.8 %psum.15 = f32[5120]{0:T(1024)S(1)} all-reduce(f32[5120]{0:T(1024)S(1)} %pad_maximum_fusion.2), channel_id=1, replica_groups=mesh['dp'=2,'ctx'=32,'tp'=8] {'dp','ctx'}, use_global_device_ids=true, to_apply=%region_2.3 | all-reduce | flops 5120 | bytes 40960 | tf_op jit(solution)/shard_map/psum | solution.py:323
  425.7 0.6 fusion.6
  426.2 0.6 slice_bitcast_fusion
  426.9 0.0 all-to-all-done.1
  426.9 0.3 copy.49
  427.2 0.8 copy.50
  428.0 0.8 copy.51
  428.7 0.8 copy.52
  429.5 0.8 copy.53
  (14 shorter events, 0.1 us)
Async XLA Ops:
  7.2 73.1 %all-gather.6.cloned.1.call-start = ((), (), s32[]{:S(2)}) async-start(), calls=%async_computation.2 | async-start | bytes 2359296 | tf_op jit(solution)/shard_map/all_gather | solution.py:253
  11.4 23.5 %copy-start = (bf16[1,128,512]{2,1,0:T(8,128)(2,1)S(1)}, bf16[1,128,512]{2,1,0:T(8,128)(2,1)}, u32[]{:S(2)}) copy-start(bf16[1,128,512]{2,1,0:T(8,128)(2,1)} %param.12) | copy-start | bytes 393220
  11.4 23.5 %copy-start.1 = (bf16[1,128,512]{2,1,0:T(8,128)(2,1)S(1)}, bf16[1,128,512]{2,1,0:T(8,128)(2,1)}, u32[]{:S(2)}) copy-start(bf16[1,128,512]{2,1,0:T(8,128)(2,1)} %param.14) | copy-start | bytes 393220
  11.4 27.0 %copy-start.6 = (f32[32,128]{1,0:T(8,128)S(1)}, f32[32,128]{1,0:T(8,128)}, u32[]{:S(2)}) copy-start(f32[32,128]{1,0:T(8,128)} %param.16) | copy-start | bytes 49156
  34.2 89.1 %all-gather.8.cloned.1.call-start = ((), (), s32[]{:S(2)}) async-start(), calls=%async_computation.3 | async-start | bytes 2359296 | tf_op jit(solution)/shard_map/all_gather | solution.py:254
  35.0 6.0 %collective-permute-start = (bf16[128,512]{1,0:T(8,128)(2,1)S(1)}, bf16[128,512]{1,0:T(8,128)(2,1)S(1)}, u32[]{:S(2)}, u32[]{:S(2)}) collective-permute-start(bf16[128,512]{1,0:T(8,128)(2,1)S(1)} %multiply_convert_fusion), channel_id=1, source_target_pairs={{0,8},{8,16},{16,24},{24,32},{32,40},{40,48},{48,56},{56,64},{64,7... | collective-permute-start | bytes 393224 | tf_op jit(solution)/shard_map/ppermute | solution.py:21
  41.0 0.7 copy-start.2
  71.6 64.2 %collective-permute-start.1 = (bf16[128,512]{1,0:T(8,128)(2,1)}, bf16[128,512]{1,0:T(8,128)(2,1)S(1)}, u32[]{:S(2)}, u32[]{:S(2)}) collective-permute-start(bf16[128,512]{1,0:T(8,128)(2,1)} %get-tuple-element.33.gated_ref), channel_id=1, source_target_pairs={{8,0},{16,8},{24,16},{32,24},{40,32},{48,40},{56,48},{64,56},{72,6... | collective-permute-start | bytes 393224 | tf_op jit(solution)/shard_map/ppermute | solution.py:21
  123.2 5.4 %copy-start.4 = (bf16[4,128,128]{2,1,0:T(8,128)(2,1)S(1)}, bf16[4,128,128]{2,1,0:T(8,128)(2,1)}, u32[]{:S(2)}) copy-start(bf16[4,128,128]{2,1,0:T(8,128)(2,1)} %get-tuple-element.41) | copy-start | bytes 393220
  123.2 5.4 %copy-start.5 = (bf16[4,128,128]{2,1,0:T(8,128)(2,1)S(1)}, bf16[4,128,128]{2,1,0:T(8,128)(2,1)}, u32[]{:S(2)}) copy-start(bf16[4,128,128]{2,1,0:T(8,128)(2,1)} %get-tuple-element.42) | copy-start | bytes 393220
  128.7 15.5 %copy-start.7 = (f32[1,512]{1,0:T(1,128)S(1)}, f32[1,512]{1,0:T(1,128)}, u32[]{:S(2)}) copy-start(f32[1,512]{1,0:T(1,128)} %get-tuple-element.40) | copy-start | bytes 6148
  130.5 296.3 %all-to-all-start.1 = ((bf16[4,4,128,128]{3,2,1,0:T(8,128)(2,1)}), bf16[4,4,128,128]{3,2,1,0:T(8,128)(2,1)S(1)}, u32[]{:S(2)}, u32[]{:S(2)}) async-start(bf16[4,4,128,128]{3,2,1,0:T(8,128)(2,1)} %copy.48), calls=%async_computation.1 | async-start | bytes 1048576 | tf_op jit(solution)/shard_map/all_to_all | solution.py:357
  135.8 0.7 copy-start.3
Sparse Core Ops, SparseCore 0:
  34.3 45.9 all-gather.5
  82.4 40.8 all-gather.7

commit v2 on v1

--- a/solution.py
+++ b/solution.py
@@ -100,7 +100,7 @@
         dq_ref[zq] = (grads[zq] * (inverses[zq] * HEAD_DIM ** (-0.5))).astype(BF16)
 
 
-def key_kernel(place_ref, own_ref, qd_ref, stat_ref, dk_ref, dv_ref):
+def key_kernel(place_ref, own_ref, qd_ref, stat_ref, att_ref, dq_ref, out_ref):
     place = place_ref[0]
     ring, strips, _, rows, depth = qd_ref.shape
     span = ring * rows
@@ -133,8 +133,10 @@
             value_sums[zk] = value_sums[zk] + value_added[lines]
             key_sums[zk] = key_sums[zk] + key_added[lines]
     for zk in range(strips):
-        dk_ref[zk] = (key_sums[zk] * HEAD_DIM ** (-0.5)).astype(BF16)
-        dv_ref[zk] = value_sums[zk].astype(BF16)
+        out_ref[zk, 0] = att_ref[zk]
+        out_ref[zk, 1] = dq_ref[zk]
+        out_ref[zk, 2] = (key_sums[zk] * HEAD_DIM ** (-0.5)).astype(BF16)
+        out_ref[zk, 3] = value_sums[zk].astype(BF16)
 
 
 def fill_phases(first, second, ext_ref, phase_ref):
@@ -215,6 +217,71 @@
         )
 
 
+def pack_kernel(*refs):
+    out_ref = refs[-1]
+    for h in range(out_ref.shape[0]):
+        for number, ref in enumerate(refs[:-1]):
+            out_ref[h, number] = ref[:, h * HEAD_DIM : (h + 1) * HEAD_DIM]
+
+
+def unpack_kernel(in_ref, *refs):
+    for h in range(in_ref.shape[0]):
+        for number, ref in enumerate(refs):
+            ref[:, h * HEAD_DIM : (h + 1) * HEAD_DIM] = in_ref[h, number]
+
+
+def exchange_kernel(x_ref, out_ref, slots_ref, send_sem, recv_sem, *, team, summed):
+    count = slots_ref.shape[0]
+    me, device = team()
+    barrier = pltpu.get_barrier_semaphore()
+    for step in range(1, count):
+        pl.semaphore_signal(
+            barrier,
+            inc=1,
+            device_id=device(lax.rem(me + step, count)),
+            device_id_type=pl.DeviceIdType.MESH,
+        )
+    slots_ref[me] = x_ref[...]
+    pl.semaphore_wait(barrier, count - 1)
+    copies = []
+    for step in range(1, count):
+        copy = pltpu.make_async_remote_copy(
+            src_ref=x_ref,
+            dst_ref=slots_ref.at[me],
+            send_sem=send_sem.at[step - 1],
+            recv_sem=recv_sem.at[step - 1],
+            device_id=device(lax.rem(me + step, count)),
+            device_id_type=pl.DeviceIdType.MESH,
+        )
+        copy.start()
+        copies.append(copy)
+    for copy in copies:
+        copy.wait()
+    if summed:
+        total = slots_ref[0]
+        for slot in range(1, count):
+            total = total + slots_ref[slot]
+        out_ref[...] = total
+    else:
+        out_ref[...] = slots_ref[...]
+
+
+def exchange(x, count, team, summed, number, name):
+    return pl.pallas_call(
+        lambda *refs: exchange_kernel(*refs, team=team, summed=summed),
+        in_specs=whole(1),
+        out_specs=whole(1)[0],
+        out_shape=shape_of(x.shape if summed else (count, *x.shape), x.dtype),
+        scratch_shapes=[
+            VMEM((count, *x.shape), x.dtype),
+            pltpu.SemaphoreType.DMA((count - 1,)),
+            pltpu.SemaphoreType.DMA((count - 1,)),
+        ],
+        compiler_params=pltpu.CompilerParams(collective_id=number, has_side_effects=True),
+        name=name,
+    )(x)
+
+
 def shape_of(shape, dtype):
     return jax.ShapeDtypeStruct(shape, dtype)
 
@@ -246,8 +313,30 @@
     across = [[strip * ring + spot for strip in range(heads)] for spot in range(ring)]
     along = [[strip * ring + spot for spot in range(ring)] for strip in range(heads)]
 
-    stacked = jnp.stack([attn_keys[0], attn_values[0], attn_queries[0], attended_grad[0]])
-    stacked = stacked.reshape(4, rows, heads, HEAD_DIM).transpose(2, 0, 1, 3)
+    lanes = lax.axis_size("tp")
+    strips = devices // ring
+
+    def over_tp():
+        return lax.axis_index("tp"), lambda peer: {"tp": peer}
+
+    def over_ring():
+        here = lax.axis_index("ctx")
+        first = here // ring * ring
+        return here % ring, lambda peer: {"ctx": first + peer}
+
+    def over_strips():
+        here = lax.axis_index("ctx")
+        spot = here % ring
+        me = lax.axis_index("dp") * strips + here // ring
+        return me, lambda peer: {"dp": peer // strips, "ctx": peer % strips * ring + spot}
+
+    stacked = pl.pallas_call(
+        pack_kernel,
+        in_specs=whole(4),
+        out_specs=whole(1)[0],
+        out_shape=shape_of((heads, 4, rows, HEAD_DIM), BF16),
+        name="pack",
+    )(attn_keys[0], attn_values[0], attn_queries[0], attended_grad[0])
     own = lax.all_to_all(stacked, "ctx", 0, 0, axis_index_groups=across, tiled=True)
     own_kv, own_qd = (own[:, :2], own[:, 2:])
     all_kv = lax.all_gather(own_kv, "ctx", axis=0, axis_index_groups=along, tiled=False)
@@ -281,7 +370,7 @@
         ),
         name="mix",
     )(left, value, before, gate, residual[0], upstream, taps_rows, skip, gain)
-    totals = lax.psum(jnp.sum(sums, axis=2), "tp").T
+    totals = exchange(jnp.sum(sums, axis=2), lanes, over_tp, True, 0, "tp_sums").T
     normed, grad_residual, grad_outer, gated, gain_part = pl.pallas_call(
         lambda *refs: norm_kernel(*refs, width=width),
         in_specs=whole(6),
@@ -320,7 +409,10 @@
     small = jnp.concatenate(
         [filter_part.reshape(-1), skip_part.reshape(-1), gain_part.reshape(-1)]
     )
-    small = lax.psum(small, ("dp", "ctx"))
+    small = exchange(small.reshape(-1, LANES), ring, over_ring, True, 1, "ring_sums")
+    small = exchange(
+        small, strips * lax.axis_size("dp"), over_strips, True, 2, "strip_sums"
+    ).reshape(-1)
     cut = groups * taps
     filter_sum = small[:cut].reshape(groups, taps)
     skip_sum, gain_sum = (small[cut : cut + channels], small[cut + channels :])
@@ -342,20 +434,25 @@
         ),
         name="query",
     )(place, own_qd, all_kv)
-    all_stats = lax.all_gather(stats, "ctx", axis=0, axis_index_groups=along, tiled=False)
-    grad_keys, grad_values = pl.pallas_call(
+    all_stats = exchange(stats, ring, over_ring, False, 3, "stats")
+    back = pl.pallas_call(
         key_kernel,
-        in_specs=[smem] + whole(3),
-        out_specs=whole(2),
-        out_shape=[shape_of(blocks, BF16)] * 2,
+        in_specs=[smem] + whole(5),
+        out_specs=whole(1)[0],
+        out_shape=shape_of((heads, 4, rows, HEAD_DIM), BF16),
         cost_estimate=pl.CostEstimate(
             flops=8 * HEAD_DIM * pairs, bytes_accessed=3 << 20, transcendentals=pairs
         ),
         name="key",
-    )(place, own_kv, all_qd, all_stats)
-    back = jnp.stack([attended, grad_queries, grad_keys, grad_values], axis=1)
+    )(place, own_kv, all_qd, all_stats, attended, grad_queries)
     back = lax.all_to_all(back, "ctx", 0, 0, axis_index_groups=across, tiled=True)
-    back = back.transpose(1, 2, 0, 3).reshape(4, rows, heads * HEAD_DIM)
+    back = pl.pallas_call(
+        unpack_kernel,
+        in_specs=whole(1),
+        out_specs=whole(4),
+        out_shape=[shape_of((rows, heads * HEAD_DIM), BF16)] * 4,
+        name="unpack",
+    )(back)
     return (
         normed[None],
         grad_left[None],
@@ -365,10 +462,10 @@
         filter_sum,
         skip_sum,
         gain_sum,
-        back[0:1],
-        back[1:2],
-        back[2:3],
-        back[3:4],
+        back[0][None],
+        back[1][None],
+        back[2][None],
+        back[3][None],
     )
 
 

time: 438 us -> 214 us (0.49)
  blocking collectives: 351 us -> 21.7 us
  waiting for transfers between devices: 20.5 us -> 82.3 us
  Pallas kernels: 24.7 us -> 73.2 us
  local copies, waits for them, and re-layouts: 13 us -> 7.88 us
    psum x2 -> x0, blocking collectives: 303 us -> none  [the longest x1 281 us: shards(): small = lax.psum(small, ('dp', 'ctx'))]
    pallas_call x1 -> x7, Pallas kernels: 5.41 us -> 53.8 us  [the longest x4 44.4 us: exchange(): pl.pallas_call(lambda *refs: exchange_kernel(*refs, team=team, summed=sum...]
    all_gather x1, waiting for transfers between devices: 7.41 us -> 44.6 us  [shards(): lax.all_gather(own_kv, 'ctx', axis=0, axis_index_groups=along, tiled=False)]
    all_gather x1 -> x0, blocking collectives: 26.1 us -> none  [shards(): lax.all_gather(stats, 'ctx', axis=0, axis_index_groups=along, tiled=False)]
    all_gather x1, waiting for transfers between devices: 10.7 us -> 28.3 us  [shards(): lax.all_gather(own_qd, 'ctx', axis=0, axis_index_groups=along, tiled=False)]
    ppermute x2, waiting for transfers between devices: 1.61 us -> 8.64 us  [passed_along(): lax.ppermute(value, axis, [(source, source + steps) for source in range(i...]
    unnamed x24 -> x12, local copies, waits for them, and re-layouts: 8.51 us -> 2.11 us
  transfers between devices with their start and end apart: 5 -> 5, of which waited for: 3 -> 4; matrix products, arithmetic and copies ran while one was open for 2% -> 4% of each run, Pallas kernels for 6% -> 30%
where the time goes in v2:
time: 214 us; the launch traced here: 213 us
  waiting for transfers between devices  82.3 us (38%)
  Pallas kernels  73.2 us (34%)
  blocking collectives  21.7 us (10%)
  between operations  14.2 us (7%)
  starting transfers between devices  9.68 us (5%)
  local copies, waits for them, and re-layouts  7.88 us (4%)
  other arithmetic  2.93 us (1%)
    all_gather x1, waiting for transfers between devices, shards(): lax.all_gather(own_kv, 'ctx', axis=0, axis_index_groups=along, tiled=False)  44.6 us
    pallas_call x4, Pallas kernels, exchange(): pl.pallas_call(lambda *refs: exchange_kernel(*refs, team=team, summed=sum...  44.4 us
    all_gather x1, waiting for transfers between devices, shards(): lax.all_gather(own_qd, 'ctx', axis=0, axis_index_groups=along, tiled=False)  28.3 us
    all_to_all x1, blocking collectives, shards(): lax.all_to_all(stacked, 'ctx', 0, 0, axis_index_groups=across, tiled=True)  21.7 us
    ppermute x2, waiting for transfers between devices, passed_along(): lax.ppermute(value, axis, [(source, source + steps) for source in range(i...  8.64 us
    pallas_call x1, Pallas kernels, shards(): pl.pallas_call(back_kernel, grid=grid, in_specs=[block] * 5 + [tap_block,...  6.49 us
    pallas_call x1, Pallas kernels, shards(): pl.pallas_call(query_kernel, in_specs=[smem] + whole(2), out_specs=whole(...  6.11 us
    pallas_call x1, Pallas kernels, shards(): pl.pallas_call(key_kernel, in_specs=[smem] + whole(5), out_specs=whole(1)...  5.58 us
  transfers between devices with their start and end apart: 5, of which 4 were waited for; matrix products, arithmetic and copies ran while one was open for 4% of the time, Pallas kernels for 30%

profile of v2, /device:TPU:2, one launch (start us, length us, event | category | flops | bytes accessed | tf_op | source)
XLA Modules:
  0.0 213.1 jit_solution(9129532898360222213)
XLA Ops:
  7.2 0.0 all-gather.7.cloned.1.call-start
  7.2 2.0 pack.1
  9.2 21.7 %all_to_all.10 = bf16[4,4,128,128]{3,2,1,0:T(8,128)(2,1)S(1)} all-to-all(bf16[4,4,128,128]{3,2,1,0:T(8,128)(2,1)} %pack.1), channel_id=1, replica_groups={{0,64,128,192},{8,72,136,200},{16,80,144,208},{24,88,152,216},{32,96,16..., dimensions={0} | all-to-all | bytes 1048576 | tf_op jit(solution)/shard_map/all_to_all | solution.py:340
  30.9 0.9 fusion.4
  31.8 0.0 all-gather.7.cloned.1.call-update
  31.8 0.0 all-gather.5.cloned.1.call-start
  31.9 0.7 all-gather.5.cloned.1.call-update
  32.6 44.6 %all-gather.7.cloned.1.call-done = bf16[32,2,128,128]{3,2,1,0:T(8,128)(2,1)} async-done(((bf16[4,2,128,128]{3,2,1,0:T(8,128)(2,1)}), bf16[32,2,128,128]{3,2,1,0:T(8,128)(2,1)}) %all-gather.7.cloned.1.call-update) | async-done | bytes 2097168 | tf_op jit(solution)/shard_map/all_gather | solution.py:342
  77.2 6.1 %query.1 = (bf16[4,128,128]{2,1,0:T(8,128)(2,1)}, bf16[4,128,128]{2,1,0:T(8,128)(2,1)}, f32[4,2,128]{2,1,0:T(2,128)}) custom-call(s32[1]{0:T(128)} %bitcast.21.place_ref, bf16[4,2,128,128]{3,2,1,0:T(8,128)(2,1)} %get-tuple-element.50.own_ref, bf16[8,4,2,128,128]{4,3,2,1,0:T(8,128)(2,1)} %bitcast.61), custom_call_target="tpu_custom_call" | custom-call | flops 1342177280 | bytes 3145728 | tf_op jit(solution)/shard_map/query/pallas_call | solution.py:423
  83.3 9.8 %stats.1.stat_ref = f32[8,4,2,128]{3,2,1,0:T(2,128)} custom-call(f32[4,2,128]{2,1,0:T(2,128)} %get-tuple-element.43.refs_0_), custom_call_target="tpu_custom_call" | custom-call | tf_op jit(solution)/shard_map/stats/pallas_call | solution.py:270
  93.1 28.3 %all-gather.5.cloned.1.call-done = bf16[32,2,128,128]{3,2,1,0:T(8,128)(2,1)} async-done(((bf16[4,2,128,128]{3,2,1,0:T(8,128)(2,1)}), bf16[32,2,128,128]{3,2,1,0:T(8,128)(2,1)}) %all-gather.5.cloned.1.call-update) | async-done | bytes 2097168 | tf_op jit(solution)/shard_map/all_gather | solution.py:343
  121.5 0.0 copy-start.1
  121.5 0.0 copy-start.2
  121.5 0.0 copy-start.5
  121.5 5.6 %key.1 = bf16[4,4,128,128]{3,2,1,0:T(8,128)(2,1)} custom-call(s32[1]{0:T(128)} %bitcast.21.place_ref, bf16[4,2,128,128]{3,2,1,0:T(8,128)(2,1)} %get-tuple-element.51.own_ref, bf16[8,4,2,128,128]{4,3,2,1,0:T(8,128)(2,1)} %bitcast.62, f32[8,4,2,128]{3,2,1,0:T(2,128)} %stats.1.stat_ref, bf16[4,128,128]{2,1,0:T(8,128)(2,1)} %get-tuple-element.44.att_ref, ...), custom_call_target="tpu_custom_call" | custom-call | flops 1342177280 | bytes 3145728 | tf_op jit(solution)/shard_map/key/pallas_call | solution.py:438
  127.1 5.1 %all-to-all-start.1 = ((bf16[4,4,128,128]{3,2,1,0:T(8,128)(2,1)}), bf16[4,4,128,128]{3,2,1,0:T(8,128)(2,1)S(1)}, u32[]{:S(2)}, u32[]{:S(2)}) async-start(bf16[4,4,128,128]{3,2,1,0:T(8,128)(2,1)} %key.1), calls=%async_computation.1 | async-start | bytes 1048576 | tf_op jit(solution)/shard_map/all_to_all | solution.py:448
  132.1 0.0 copy-done.1
  132.1 0.0 copy-done.2
  132.2 3.2 %collective-permute-start = (bf16[128,512]{1,0:T(8,128)(2,1)S(1)}, bf16[128,512]{1,0:T(8,128)(2,1)S(1)}, u32[]{:S(2)}, u32[]{:S(2)}) collective-permute-start(bf16[128,512]{1,0:T(8,128)(2,1)S(1)} %multiply_convert_fusion), channel_id=1, source_target_pairs={{0,8},{8,16},{16,24},{24,32},{32,40},{40,48},{48,56},{56,64},{64,7... | collective-permute-start | bytes 393224 | tf_op jit(solution)/shard_map/ppermute | solution.py:21
  135.4 0.0 copy-done.5
  135.5 0.8 copy.29.taps_ref
  136.3 1.6 collective-permute-done.before_ref
  137.9 0.0 copy-start.3
  137.9 0.7 copy-done.3
  138.6 4.6 %mix.1 = (f32[128,512]{1,0:T(8,128)}, f32[128,512]{1,0:T(8,128)}, f32[2,128,128]{2,1,0:T(8,128)}) custom-call(bf16[128,512]{1,0:T(8,128)(2,1)} %bitcast.39, bf16[128,512]{1,0:T(8,128)(2,1)} %bitcast.41, bf16[128,512]{1,0:T(8,128)(2,1)} %copy-done.3, bf16[128,512]{1,0:T(8,128)(2,1)} %bitcast.46, bf16[128,512]{1,0:T(8,128)(2,1)} %bitcast.53, ...), custom_call_target="tpu_custom_call" | custom-call | flops 16777216 | bytes 1310720 | tf_op jit(solution)/shard_map/mix/pallas_call | solution.py:357
  143.2 1.6 reduce_sum.9.refs_0_
  144.8 7.2 %tp_sums.1 = f32[2,128]{1,0:T(2,128)} custom-call(f32[2,128]{1,0:T(2,128)} %reduce_sum.9.refs_0_), custom_call_target="tpu_custom_call" | custom-call | tf_op jit(solution)/shard_map/tp_sums/pallas_call | solution.py:270
  151.9 1.4 copy.30
  153.3 2.1 norm.1
  155.5 1.3 collective-permute-start.1
  156.8 7.0 %collective-permute-done.1.after_ref = bf16[128,512]{1,0:T(8,128)(2,1)S(1)} collective-permute-done((bf16[128,512]{1,0:T(8,128)(2,1)}, bf16[128,512]{1,0:T(8,128)(2,1)S(1)}, u32[]{:S(2)}, u32[]{:S(2)}) %collective-permute-start.1) | collective-permute-done | bytes 131104 | tf_op jit(solution)/shard_map/ppermute | solution.py:21
  163.8 0.0 copy-start.4
  163.8 0.7 copy-done.4
  164.4 6.5 %back.1 = (bf16[128,512]{1,0:T(8,128)(2,1)}, bf16[128,512]{1,0:T(8,128)(2,1)}, f32[128,512]{1,0:T(8,128)}, f32[1,512]{1,0:T(1,128)}) custom-call(bf16[128,512]{1,0:T(8,128)(2,1)} %bitcast.40, bf16[128,512]{1,0:T(8,128)(2,1)} %bitcast.42, bf16[128,512]{1,0:T(8,128)(2,1)} %copy-done.3, bf16[128,512]{1,0:T(8,128)(2,1)} %get-tuple-element.35.gated_ref, ...), custom_call_target="tpu_custom_call" | custom-call | flops 33554432 | bytes 1310720 | tf_op jit(solution)/shard_map/back/pallas_call | solution.py:385
  170.9 1.2 convolution_bitcast_fusion
  172.1 1.3 maximum_bitcast_fusion.refs_0_
  173.5 13.9 %ring_sums.1.refs_0_ = f32[40,128]{1,0:T(8,128)} custom-call(f32[40,128]{1,0:T(8,128)} %maximum_bitcast_fusion.refs_0_), custom_call_target="tpu_custom_call" | custom-call | tf_op jit(solution)/shard_map/ring_sums/pallas_call | solution.py:270
  187.4 13.5 %strip_sums.1 = f32[40,128]{1,0:T(8,128)} custom-call(f32[40,128]{1,0:T(8,128)} %ring_sums.1.refs_0_), custom_call_target="tpu_custom_call" | custom-call | tf_op jit(solution)/shard_map/strip_sums/pallas_call | solution.py:270
  200.9 1.3 slice.22
  202.2 1.3 slice_bitcast_fusion
  203.6 0.0 all-to-all-done.1.in_ref
  203.6 0.0 copy-start
  203.6 0.8 copy-done
  204.3 1.9 unpack.1
  (3 shorter events, 0.1 us)
Async XLA Ops:
  7.2 70.1 %all-gather.7.cloned.1.call-start = ((), (), s32[]{:S(2)}) async-start(), calls=%async_computation.3 | async-start | bytes 2359296 | tf_op jit(solution)/shard_map/all_gather | solution.py:342
  31.8 89.6 %all-gather.5.cloned.1.call-start = ((), (), s32[]{:S(2)}) async-start(), calls=%async_computation.2 | async-start | bytes 2359296 | tf_op jit(solution)/shard_map/all_gather | solution.py:343
  121.5 10.7 %copy-start.1 = (bf16[1,128,512]{2,1,0:T(8,128)(2,1)S(1)}, bf16[1,128,512]{2,1,0:T(8,128)(2,1)}, u32[]{:S(2)}) copy-start(bf16[1,128,512]{2,1,0:T(8,128)(2,1)} %param.12) | copy-start | bytes 393220
  121.5 10.7 %copy-start.2 = (bf16[1,128,512]{2,1,0:T(8,128)(2,1)S(1)}, bf16[1,128,512]{2,1,0:T(8,128)(2,1)}, u32[]{:S(2)}) copy-start(bf16[1,128,512]{2,1,0:T(8,128)(2,1)} %param.14) | copy-start | bytes 393220
  121.5 14.0 %copy-start.5 = (f32[32,128]{1,0:T(8,128)S(1)}, f32[32,128]{1,0:T(8,128)}, u32[]{:S(2)}) copy-start(f32[32,128]{1,0:T(8,128)} %param.16) | copy-start | bytes 49156
  127.1 76.5 %all-to-all-start.1 = ((bf16[4,4,128,128]{3,2,1,0:T(8,128)(2,1)}), bf16[4,4,128,128]{3,2,1,0:T(8,128)(2,1)S(1)}, u32[]{:S(2)}, u32[]{:S(2)}) async-start(bf16[4,4,128,128]{3,2,1,0:T(8,128)(2,1)} %key.1), calls=%async_computation.1 | async-start | bytes 1048576 | tf_op jit(solution)/shard_map/all_to_all | solution.py:448
  132.2 5.7 %collective-permute-start = (bf16[128,512]{1,0:T(8,128)(2,1)S(1)}, bf16[128,512]{1,0:T(8,128)(2,1)S(1)}, u32[]{:S(2)}, u32[]{:S(2)}) collective-permute-start(bf16[128,512]{1,0:T(8,128)(2,1)S(1)} %multiply_convert_fusion), channel_id=1, source_target_pairs={{0,8},{8,16},{16,24},{24,32},{32,40},{40,48},{48,56},{56,64},{64,7... | collective-permute-start | bytes 393224 | tf_op jit(solution)/shard_map/ppermute | solution.py:21
  137.9 0.7 copy-start.3
  155.5 8.3 %collective-permute-start.1 = (bf16[128,512]{1,0:T(8,128)(2,1)}, bf16[128,512]{1,0:T(8,128)(2,1)S(1)}, u32[]{:S(2)}, u32[]{:S(2)}) collective-permute-start(bf16[128,512]{1,0:T(8,128)(2,1)} %get-tuple-element.35.gated_ref), channel_id=1, source_target_pairs={{8,0},{16,8},{24,16},{32,24},{40,32},{48,40},{56,48},{64,56},{72,6... | collective-permute-start | bytes 393224 | tf_op jit(solution)/shard_map/ppermute | solution.py:21
  163.8 0.7 copy-start.4
  203.6 0.8 copy-start
Sparse Core Ops, SparseCore 0:
  32.0 45.2 all-gather.6
  79.3 42.0 all-gather.4

commit v3 on v2

--- a/solution.py
+++ b/solution.py
@@ -217,11 +217,13 @@
         )
 
 
-def pack_kernel(*refs):
-    out_ref = refs[-1]
-    for h in range(out_ref.shape[0]):
-        for number, ref in enumerate(refs[:-1]):
-            out_ref[h, number] = ref[:, h * HEAD_DIM : (h + 1) * HEAD_DIM]
+def pack_kernel(key_ref, value_ref, query_ref, grad_ref, kv_ref, qd_ref):
+    for h in range(kv_ref.shape[0]):
+        columns = slice(h * HEAD_DIM, (h + 1) * HEAD_DIM)
+        kv_ref[h, 0] = key_ref[:, columns]
+        kv_ref[h, 1] = value_ref[:, columns]
+        qd_ref[h, 0] = query_ref[:, columns]
+        qd_ref[h, 1] = grad_ref[:, columns]
 
 
 def unpack_kernel(in_ref, *refs):
@@ -330,18 +332,21 @@
         me = lax.axis_index("dp") * strips + here // ring
         return me, lambda peer: {"dp": peer // strips, "ctx": peer % strips * ring + spot}
 
-    stacked = pl.pallas_call(
+    pair = shape_of((heads, 2, rows, HEAD_DIM), BF16)
+    send_kv, send_qd = pl.pallas_call(
         pack_kernel,
         in_specs=whole(4),
-        out_specs=whole(1)[0],
-        out_shape=shape_of((heads, 4, rows, HEAD_DIM), BF16),
+        out_specs=whole(2),
+        out_shape=[pair, pair],
         name="pack",
     )(attn_keys[0], attn_values[0], attn_queries[0], attended_grad[0])
-    own = lax.all_to_all(stacked, "ctx", 0, 0, axis_index_groups=across, tiled=True)
-    own_kv, own_qd = (own[:, :2], own[:, 2:])
+    own_kv = lax.all_to_all(send_kv, "ctx", 0, 0, axis_index_groups=across, tiled=True)
     all_kv = lax.all_gather(own_kv, "ctx", axis=0, axis_index_groups=along, tiled=False)
+    own_kv, send_qd = lax.optimization_barrier((own_kv, send_qd))
+    own_qd = lax.all_to_all(send_qd, "ctx", 0, 0, axis_index_groups=across, tiled=True)
     all_qd = lax.all_gather(own_qd, "ctx", axis=0, axis_index_groups=along, tiled=False)
 
+    own_qd, left_stream = lax.optimization_barrier((own_qd, left_stream))
     left, value, gate = (left_stream[0], value_stream[0], outer_gate[0])
     upstream = normed_grad[0]
     product = (left.astype(F32) * value.astype(F32)).astype(BF16)
@@ -409,10 +414,12 @@
     small = jnp.concatenate(
         [filter_part.reshape(-1), skip_part.reshape(-1), gain_part.reshape(-1)]
     )
-    small = exchange(small.reshape(-1, LANES), ring, over_ring, True, 1, "ring_sums")
+    small, own_qd = lax.optimization_barrier((small.reshape(-1, LANES), own_qd))
+    small = exchange(small, ring, over_ring, True, 1, "ring_sums")
     small = exchange(
         small, strips * lax.axis_size("dp"), over_strips, True, 2, "strip_sums"
     ).reshape(-1)
+    small, own_kv = lax.optimization_barrier((small, own_kv))
     cut = groups * taps
     filter_sum = small[:cut].reshape(groups, taps)
     skip_sum, gain_sum = (small[cut : cut + channels], small[cut + channels :])

time: 214 us -> 158 us (0.74)
  the two profiles are of different devices: /device:TPU:2 before, /device:TPU:16 now
where the time goes in v3:
time: 158 us; the launch traced here: 157 us
  Pallas kernels  75.6 us (48%)
  blocking collectives  27.5 us (17%)
  waiting for transfers between devices  20.6 us (13%)
  between operations  14.2 us (9%)
  starting transfers between devices  9.48 us (6%)
  local copies, waits for them, and re-layouts  5.61 us (4%)
  other arithmetic  2.93 us (2%)
    pallas_call x4, Pallas kernels, exchange(): pl.pallas_call(lambda *refs: exchange_kernel(*refs, team=team, summed=sum...  46.8 us
    all_to_all x1, blocking collectives, shards(): lax.all_to_all(send_kv, 'ctx', 0, 0, axis_index_groups=across, tiled=True)  16.2 us
    all_to_all x1, blocking collectives, shards(): lax.all_to_all(send_qd, 'ctx', 0, 0, axis_index_groups=across, tiled=True)  11.2 us
    ppermute x2, waiting for transfers between devices, passed_along(): lax.ppermute(value, axis, [(source, source + steps) for source in range(i...  10.4 us
    all_to_all x1, waiting for transfers between devices, shards(): lax.all_to_all(back, 'ctx', 0, 0, axis_index_groups=across, tiled=True)  10.1 us
    pallas_call x1, Pallas kernels, shards(): pl.pallas_call(back_kernel, grid=grid, in_specs=[block] * 5 + [tap_block,...  6.48 us
    pallas_call x1, Pallas kernels, shards(): pl.pallas_call(query_kernel, in_specs=[smem] + whole(2), out_specs=whole(...  6.14 us
    ppermute x2, starting transfers between devices, passed_along(): lax.ppermute(value, axis, [(source, source + steps) for source in range(i...  5.93 us
  transfers between devices with their start and end apart: 5, of which 3 were waited for; matrix products, arithmetic and copies ran while one was open for 5% of the time, Pallas kernels for 42%

profile of v3, /device:TPU:16, one launch (start us, length us, event | category | flops | bytes accessed | tf_op | source)
XLA Modules:
  0.0 157.2 jit_solution(9440205083216321597)
XLA Ops:
  7.2 0.0 copy-start.1
  7.2 0.0 copy-start.2
  7.2 0.0 copy-start.6
  7.2 0.0 all-gather.7.cloned.1.call-start
  7.3 2.0 %pack.1 = (bf16[4,2,128,128]{3,2,1,0:T(8,128)(2,1)}, bf16[4,2,128,128]{3,2,1,0:T(8,128)(2,1)}) custom-call(bf16[128,512]{1,0:T(8,128)(2,1)} %bitcast.48, bf16[128,512]{1,0:T(8,128)(2,1)} %bitcast.49, bf16[128,512]{1,0:T(8,128)(2,1)} %bitcast.50, bf16[128,512]{1,0:T(8,128)(2,1)} %bitcast.51), custom_call_target="tpu_custom_call" | custom-call | tf_op jit(solution)/shard_map/pack/pallas_call | solution.py:336
  9.3 16.2 %all_to_all.15.own_ref = bf16[4,2,128,128]{3,2,1,0:T(8,128)(2,1)} all-to-all(bf16[4,2,128,128]{3,2,1,0:T(8,128)(2,1)} %get-tuple-element.41), channel_id=1, replica_groups={{0,64,128,192},{8,72,136,200},{16,80,144,208},{24,88,152,216},{32,96,16..., dimensions={0} | all-to-all | bytes 524288 | tf_op jit(solution)/shard_map/all_to_all | solution.py:343
  25.5 0.0 all-gather.7.cloned.1.call-update
  25.6 0.0 all-gather.5.cloned.1.call-start
  25.6 11.2 %all_to_all.16.own_ref = bf16[4,2,128,128]{3,2,1,0:T(8,128)(2,1)} all-to-all(bf16[4,2,128,128]{3,2,1,0:T(8,128)(2,1)} %get-tuple-element.43), channel_id=1, replica_groups={{0,64,128,192},{8,72,136,200},{16,80,144,208},{24,88,152,216},{32,96,16..., dimensions={0} | all-to-all | bytes 524288 | tf_op jit(solution)/shard_map/all_to_all | solution.py:346
  36.8 0.0 all-gather.5.cloned.1.call-update
  36.9 0.0 copy-done.1
  36.9 0.0 copy-done.2
  36.9 3.5 %collective-permute-start = (bf16[128,512]{1,0:T(8,128)(2,1)S(1)}, bf16[128,512]{1,0:T(8,128)(2,1)S(1)}, u32[]{:S(2)}, u32[]{:S(2)}) collective-permute-start(bf16[128,512]{1,0:T(8,128)(2,1)S(1)} %multiply_convert_fusion), channel_id=1, source_target_pairs={{0,8},{8,16},{16,24},{24,32},{32,40},{40,48},{48,56},{56,64},{64,7... | collective-permute-start | bytes 393224 | tf_op jit(solution)/shard_map/ppermute | solution.py:21
  40.4 0.0 copy-done.6
  40.5 0.8 copy.29.taps_ref
  41.3 5.1 %collective-permute-done.before_ref = bf16[128,512]{1,0:T(8,128)(2,1)S(1)} collective-permute-done((bf16[128,512]{1,0:T(8,128)(2,1)S(1)}, bf16[128,512]{1,0:T(8,128)(2,1)S(1)}, u32[]{:S(2)}, u32[]{:S(2)}) %collective-permute-start) | collective-permute-done | bytes 131104 | tf_op jit(solution)/shard_map/ppermute | solution.py:21
  46.4 0.0 copy-start.3
  46.4 0.7 copy-done.3
  47.1 4.6 %mix.1 = (f32[128,512]{1,0:T(8,128)}, f32[128,512]{1,0:T(8,128)}, f32[2,128,128]{2,1,0:T(8,128)}) custom-call(bf16[128,512]{1,0:T(8,128)(2,1)} %bitcast.38, bf16[128,512]{1,0:T(8,128)(2,1)} %bitcast.40, bf16[128,512]{1,0:T(8,128)(2,1)} %copy-done.3, bf16[128,512]{1,0:T(8,128)(2,1)} %bitcast.45, bf16[128,512]{1,0:T(8,128)(2,1)} %bitcast.52, ...), custom_call_target="tpu_custom_call" | custom-call | flops 16777216 | bytes 1310720 | tf_op jit(solution)/shard_map/mix/pallas_call | solution.py:362
  51.7 1.6 %reduce_sum.9.refs_0_ = f32[2,128]{1,0:T(2,128)} reduce(f32[2,128,128]{2,1,0:T(8,128)} %get-tuple-element.47, f32[]{:T(128)} %constant.28.clone.1), dimensions={2}, to_apply=%region_0.1 | reduce | flops 32512 | bytes 132100 | tf_op jit(solution)/shard_map/reduce_sum | solution.py:378
  53.3 7.8 %tp_sums.1 = f32[2,128]{1,0:T(2,128)} custom-call(f32[2,128]{1,0:T(2,128)} %reduce_sum.9.refs_0_), custom_call_target="tpu_custom_call" | custom-call | tf_op jit(solution)/shard_map/tp_sums/pallas_call | solution.py:272
  61.1 1.4 copy.30
  62.5 2.1 %norm.1 = (bf16[128,512]{1,0:T(8,128)(2,1)}, bf16[128,512]{1,0:T(8,128)(2,1)}, bf16[128,512]{1,0:T(8,128)(2,1)}, bf16[128,512]{1,0:T(8,128)(2,1)}, f32[1,512]{1,0:T(1,128)}) custom-call(bf16[128,512]{1,0:T(8,128)(2,1)} %bitcast.44, bf16[128,512]{1,0:T(8,128)(2,1)} %bitcast.46, f32[128,512]{1,0:T(8,128)} %get-tuple-element.45.refs_2_, ...), custom_call_target="tpu_custom_call" | custom-call | flops 1310720 | bytes 1310720 | tf_op jit(solution)/shard_map/norm/pallas_call | solution.py:379
  64.6 2.4 %collective-permute-start.1 = (bf16[128,512]{1,0:T(8,128)(2,1)}, bf16[128,512]{1,0:T(8,128)(2,1)S(1)}, u32[]{:S(2)}, u32[]{:S(2)}) collective-permute-start(bf16[128,512]{1,0:T(8,128)(2,1)} %get-tuple-element.49.gated_ref), channel_id=1, source_target_pairs={{8,0},{16,8},{24,16},{32,24},{40,32},{48,40},{56,48},{64,56},{72,6... | collective-permute-start | bytes 393224 | tf_op jit(solution)/shard_map/ppermute | solution.py:21
  67.1 5.3 %collective-permute-done.1.after_ref = bf16[128,512]{1,0:T(8,128)(2,1)S(1)} collective-permute-done((bf16[128,512]{1,0:T(8,128)(2,1)}, bf16[128,512]{1,0:T(8,128)(2,1)S(1)}, u32[]{:S(2)}, u32[]{:S(2)}) %collective-permute-start.1) | collective-permute-done | bytes 131104 | tf_op jit(solution)/shard_map/ppermute | solution.py:21
  72.5 0.0 copy-start.4
  72.5 0.7 copy-done.4
  73.1 6.5 %back.1 = (bf16[128,512]{1,0:T(8,128)(2,1)}, bf16[128,512]{1,0:T(8,128)(2,1)}, f32[128,512]{1,0:T(8,128)}, f32[1,512]{1,0:T(1,128)}) custom-call(bf16[128,512]{1,0:T(8,128)(2,1)} %bitcast.39, bf16[128,512]{1,0:T(8,128)(2,1)} %bitcast.41, bf16[128,512]{1,0:T(8,128)(2,1)} %copy-done.3, bf16[128,512]{1,0:T(8,128)(2,1)} %get-tuple-element.49.gated_ref, ...), custom_call_target="tpu_custom_call" | custom-call | flops 33554432 | bytes 1310720 | tf_op jit(solution)/shard_map/back/pallas_call | solution.py:390
  79.6 1.2 convolution_bitcast_fusion
  80.8 1.3 maximum_bitcast_fusion.refs_0_
  82.1 16.4 %ring_sums.1.refs_0_ = f32[40,128]{1,0:T(8,128)} custom-call(f32[40,128]{1,0:T(8,128)} %maximum_bitcast_fusion.refs_0_), custom_call_target="tpu_custom_call" | custom-call | tf_op jit(solution)/shard_map/ring_sums/pallas_call | solution.py:272
  98.5 12.6 %strip_sums.1 = f32[40,128]{1,0:T(8,128)} custom-call(f32[40,128]{1,0:T(8,128)} %ring_sums.1.refs_0_), custom_call_target="tpu_custom_call" | custom-call | tf_op jit(solution)/shard_map/strip_sums/pallas_call | solution.py:272
  111.1 0.0 all-gather.7.cloned.1.call-done
  111.2 6.1 %query.1 = (bf16[4,128,128]{2,1,0:T(8,128)(2,1)}, bf16[4,128,128]{2,1,0:T(8,128)(2,1)}, f32[4,2,128]{2,1,0:T(2,128)}) custom-call(s32[1]{0:T(128)} %bitcast.25.place_ref, bf16[4,2,128,128]{3,2,1,0:T(8,128)(2,1)} %all_to_all.16.own_ref, bf16[8,4,2,128,128]{4,3,2,1,0:T(8,128)(2,1)} %bitcast.62), custom_call_target="tpu_custom_call" | custom-call | flops 1342177280 | bytes 3145728 | tf_op jit(solution)/shard_map/query/pallas_call | solution.py:430
  117.3 9.9 %stats.1.stat_ref = f32[8,4,2,128]{3,2,1,0:T(2,128)} custom-call(f32[4,2,128]{2,1,0:T(2,128)} %get-tuple-element.63.refs_0_), custom_call_target="tpu_custom_call" | custom-call | tf_op jit(solution)/shard_map/stats/pallas_call | solution.py:272
  127.2 0.0 all-gather.5.cloned.1.call-done
  127.3 0.0 copy-start.5
  127.3 5.5 %key.1 = bf16[4,4,128,128]{3,2,1,0:T(8,128)(2,1)} custom-call(s32[1]{0:T(128)} %bitcast.25.place_ref, bf16[4,2,128,128]{3,2,1,0:T(8,128)(2,1)} %all_to_all.15.own_ref, bf16[8,4,2,128,128]{4,3,2,1,0:T(8,128)(2,1)} %bitcast.63, f32[8,4,2,128]{3,2,1,0:T(2,128)} %stats.1.stat_ref, bf16[4,128,128]{2,1,0:T(8,128)(2,1)} %get-tuple-element.64.att_ref, ...), custom_call_target="tpu_custom_call" | custom-call | flops 1342177280 | bytes 3145728 | tf_op jit(solution)/shard_map/key/pallas_call | solution.py:445
  132.8 3.5 %all-to-all-start.2 = ((bf16[4,4,128,128]{3,2,1,0:T(8,128)(2,1)}), bf16[4,4,128,128]{3,2,1,0:T(8,128)(2,1)S(1)}, u32[]{:S(2)}, u32[]{:S(2)}) async-start(bf16[4,4,128,128]{3,2,1,0:T(8,128)(2,1)} %key.1), calls=%async_computation.2 | async-start | bytes 1048576 | tf_op jit(solution)/shard_map/all_to_all | solution.py:455
  136.3 0.0 copy-done.5
  136.3 0.6 fusion.4
  136.9 0.6 slice_bitcast_fusion
  137.5 10.1 %all-to-all-done.2.in_ref = bf16[4,4,128,128]{3,2,1,0:T(8,128)(2,1)S(1)} async-done(((bf16[4,4,128,128]{3,2,1,0:T(8,128)(2,1)}), bf16[4,4,128,128]{3,2,1,0:T(8,128)(2,1)S(1)}, u32[]{:S(2)}, u32[]{:S(2)}) %all-to-all-start.2) | async-done | bytes 524320 | tf_op jit(solution)/shard_map/all_to_all | solution.py:455
  147.6 0.0 copy-start
  147.6 0.8 copy-done
  148.4 1.9 %unpack.1 = (bf16[128,512]{1,0:T(8,128)(2,1)}, bf16[128,512]{1,0:T(8,128)(2,1)}, bf16[128,512]{1,0:T(8,128)(2,1)}, bf16[128,512]{1,0:T(8,128)(2,1)}) custom-call(bf16[4,4,128,128]{3,2,1,0:T(8,128)(2,1)} %copy-done), custom_call_target="tpu_custom_call" | custom-call | tf_op jit(solution)/shard_map/unpack/pallas_call | solution.py:456
  (3 shorter events, 0.1 us)
Async XLA Ops:
  7.2 29.7 %copy-start.1 = (bf16[1,128,512]{2,1,0:T(8,128)(2,1)S(1)}, bf16[1,128,512]{2,1,0:T(8,128)(2,1)}, u32[]{:S(2)}) copy-start(bf16[1,128,512]{2,1,0:T(8,128)(2,1)} %param.12) | copy-start | bytes 393220
  7.2 29.7 %copy-start.2 = (bf16[1,128,512]{2,1,0:T(8,128)(2,1)S(1)}, bf16[1,128,512]{2,1,0:T(8,128)(2,1)}, u32[]{:S(2)}) copy-start(bf16[1,128,512]{2,1,0:T(8,128)(2,1)} %param.14) | copy-start | bytes 393220
  7.2 33.2 %copy-start.6 = (f32[32,128]{1,0:T(8,128)S(1)}, f32[32,128]{1,0:T(8,128)}, u32[]{:S(2)}) copy-start(f32[32,128]{1,0:T(8,128)} %param.16) | copy-start | bytes 49156
  7.2 103.9 %all-gather.7.cloned.1.call-start = ((), (), s32[]{:S(2)}) async-start(), calls=%async_computation.4 | async-start | bytes 2359296 | tf_op jit(solution)/shard_map/all_gather | solution.py:344
  25.6 101.7 %all-gather.5.cloned.1.call-start = ((), (), s32[]{:S(2)}) async-start(), calls=%async_computation.3 | async-start | bytes 2359296 | tf_op jit(solution)/shard_map/all_gather | solution.py:347
  36.9 9.5 %collective-permute-start = (bf16[128,512]{1,0:T(8,128)(2,1)S(1)}, bf16[128,512]{1,0:T(8,128)(2,1)S(1)}, u32[]{:S(2)}, u32[]{:S(2)}) collective-permute-start(bf16[128,512]{1,0:T(8,128)(2,1)S(1)} %multiply_convert_fusion), channel_id=1, source_target_pairs={{0,8},{8,16},{16,24},{24,32},{32,40},{40,48},{48,56},{56,64},{64,7... | collective-permute-start | bytes 393224 | tf_op jit(solution)/shard_map/ppermute | solution.py:21
  46.4 0.7 copy-start.3
  64.6 7.8 %collective-permute-start.1 = (bf16[128,512]{1,0:T(8,128)(2,1)}, bf16[128,512]{1,0:T(8,128)(2,1)S(1)}, u32[]{:S(2)}, u32[]{:S(2)}) collective-permute-start(bf16[128,512]{1,0:T(8,128)(2,1)} %get-tuple-element.49.gated_ref), channel_id=1, source_target_pairs={{8,0},{16,8},{24,16},{32,24},{40,32},{48,40},{56,48},{64,56},{72,6... | collective-permute-start | bytes 393224 | tf_op jit(solution)/shard_map/ppermute | solution.py:21
  72.5 0.7 copy-start.4
  127.3 9.0 %copy-start.5 = (f32[40,128]{1,0:T(8,128)S(1)}, f32[40,128]{1,0:T(8,128)}, u32[]{:S(2)}) copy-start(f32[40,128]{1,0:T(8,128)} %strip_sums.1) | copy-start | bytes 61444
  132.8 14.8 %all-to-all-start.2 = ((bf16[4,4,128,128]{3,2,1,0:T(8,128)(2,1)}), bf16[4,4,128,128]{3,2,1,0:T(8,128)(2,1)S(1)}, u32[]{:S(2)}, u32[]{:S(2)}) async-start(bf16[4,4,128,128]{3,2,1,0:T(8,128)(2,1)} %key.1), calls=%async_computation.2 | async-start | bytes 1048576 | tf_op jit(solution)/shard_map/all_to_all | solution.py:455
  147.6 0.8 copy-start
Sparse Core Ops, SparseCore 0:
  25.7 44.2 all-gather.6
  72.1 45.7 all-gather.4

commit v4 on v3

--- a/solution.py
+++ b/solution.py
@@ -100,8 +100,11 @@
         dq_ref[zq] = (grads[zq] * (inverses[zq] * HEAD_DIM ** (-0.5))).astype(BF16)
 
 
-def key_kernel(place_ref, own_ref, qd_ref, stat_ref, att_ref, dq_ref, out_ref):
+def key_kernel(place_ref, own_ref, stat_ref, att_ref, dq_ref, *refs):
+    *hop_refs, out_ref, qd_ref = refs
     place = place_ref[0]
+    for step, hop_ref in enumerate(hop_refs):
+        qd_ref[lax.rem(place - step + len(hop_refs), len(hop_refs))] = hop_ref[...]
     ring, strips, _, rows, depth = qd_ref.shape
     span = ring * rows
     factor = HEAD_DIM ** (-0.5) * LOG2E
@@ -344,7 +347,12 @@
     all_kv = lax.all_gather(own_kv, "ctx", axis=0, axis_index_groups=along, tiled=False)
     own_kv, send_qd = lax.optimization_barrier((own_kv, send_qd))
     own_qd = lax.all_to_all(send_qd, "ctx", 0, 0, axis_index_groups=across, tiled=True)
-    all_qd = lax.all_gather(own_qd, "ctx", axis=0, axis_index_groups=along, tiled=False)
+    hops = [own_qd]
+    for step in range(1, ring):
+        pairs = [
+            (team[spot], team[(spot + step) % ring]) for team in along for spot in range(ring)
+        ]
+        hops.append(lax.ppermute(own_qd, "ctx", pairs))
 
     own_qd, left_stream = lax.optimization_barrier((own_qd, left_stream))
     left, value, gate = (left_stream[0], value_stream[0], outer_gate[0])
@@ -415,14 +423,6 @@
         [filter_part.reshape(-1), skip_part.reshape(-1), gain_part.reshape(-1)]
     )
     small, own_qd = lax.optimization_barrier((small.reshape(-1, LANES), own_qd))
-    small = exchange(small, ring, over_ring, True, 1, "ring_sums")
-    small = exchange(
-        small, strips * lax.axis_size("dp"), over_strips, True, 2, "strip_sums"
-    ).reshape(-1)
-    small, own_kv = lax.optimization_barrier((small, own_kv))
-    cut = groups * taps
-    filter_sum = small[:cut].reshape(groups, taps)
-    skip_sum, gain_sum = (small[cut : cut + channels], small[cut + channels :])
 
     smem = pl.BlockSpec(memory_space=pltpu.SMEM)
     blocks = (heads, rows, HEAD_DIM)
@@ -441,17 +441,24 @@
         ),
         name="query",
     )(place, own_qd, all_kv)
-    all_stats = exchange(stats, ring, over_ring, False, 3, "stats")
+    lines = 2 * heads
+    gathered = exchange(
+        jnp.concatenate([stats.reshape(lines, rows), small], axis=0),
+        ring, over_ring, False, 1, "ring_gather",
+    )
+    all_stats = gathered[:, :lines].reshape(ring, heads, 2, rows)
     back = pl.pallas_call(
         key_kernel,
-        in_specs=[smem] + whole(5),
+        in_specs=[smem] + whole(4 + ring),
         out_specs=whole(1)[0],
         out_shape=shape_of((heads, 4, rows, HEAD_DIM), BF16),
+        scratch_shapes=[VMEM((ring, heads, 2, rows, HEAD_DIM), BF16)],
         cost_estimate=pl.CostEstimate(
             flops=8 * HEAD_DIM * pairs, bytes_accessed=3 << 20, transcendentals=pairs
         ),
         name="key",
-    )(place, own_kv, all_qd, all_stats, attended, grad_queries)
+    )(place, own_kv, all_stats, attended, grad_queries, *hops)
+    back, gathered = lax.optimization_barrier((back, gathered))
     back = lax.all_to_all(back, "ctx", 0, 0, axis_index_groups=across, tiled=True)
     back = pl.pallas_call(
         unpack_kernel,
@@ -460,6 +467,13 @@
         out_shape=[shape_of((rows, heads * HEAD_DIM), BF16)] * 4,
         name="unpack",
     )(back)
+    small = exchange(
+        jnp.sum(gathered[:, lines:], axis=0),
+        strips * lax.axis_size("dp"), over_strips, True, 2, "strip_sums",
+    ).reshape(-1)
+    cut = groups * taps
+    filter_sum = small[:cut].reshape(groups, taps)
+    skip_sum, gain_sum = (small[cut : cut + channels], small[cut + channels :])
     return (
         normed[None],
         grad_left[None],

time: 158 us -> 182 us (1.15)
  starting transfers between devices: 9.48 us -> 38.9 us
  waiting for transfers between devices: 20.6 us -> 0.04 us
  Pallas kernels: 75.6 us -> 84.9 us
  local copies, waits for them, and re-layouts: 5.61 us -> 8.8 us
  other arithmetic: 2.93 us -> 5.3 us
    ppermute x0 -> x7, starting transfers between devices: none -> 27.8 us  [shards(): hops.append(lax.ppermute(own_qd, 'ctx', pairs))]
    ppermute x2, waiting for transfers between devices: 10.4 us -> 0.01 us  [passed_along(): lax.ppermute(value, axis, [(source, source + steps) for source in range(i...]
    all_to_all x1, waiting for transfers between devices: 10.1 us -> 0.01 us  [shards(): lax.all_to_all(back, 'ctx', 0, 0, axis_index_groups=across, tiled=True)]
    pallas_call x4 -> x3, Pallas kernels: 46.8 us -> 55.8 us  [exchange(): pl.pallas_call(lambda *refs: exchange_kernel(*refs, team=team, summed=sum...]
  transfers between devices with their start and end apart: 5 -> 11, of which waited for: 3 -> 0; matrix products, arithmetic and copies ran while one was open for 5% -> 7% of each run, Pallas kernels for 42% -> 42%
where the time goes in v4:
time: 182 us; the launch traced here: 181 us
  Pallas kernels  84.9 us (47%)
  starting transfers between devices  38.9 us (21%)
  blocking collectives  27.4 us (15%)
  between operations  14.3 us (8%)
  local copies, waits for them, and re-layouts  8.8 us (5%)
  other arithmetic  5.3 us (3%)
    pallas_call x3, Pallas kernels, exchange(): pl.pallas_call(lambda *refs: exchange_kernel(*refs, team=team, summed=sum...  55.8 us
    ppermute x7, starting transfers between devices, shards(): hops.append(lax.ppermute(own_qd, 'ctx', pairs))  27.8 us
    all_to_all x1, blocking collectives, shards(): lax.all_to_all(send_kv, 'ctx', 0, 0, axis_index_groups=across, tiled=True)  16.2 us
    all_to_all x1, blocking collectives, shards(): lax.all_to_all(send_qd, 'ctx', 0, 0, axis_index_groups=across, tiled=True)  11.2 us
    ppermute x2, starting transfers between devices, passed_along(): lax.ppermute(value, axis, [(source, source + steps) for source in range(i...  6.73 us
    pallas_call x1, Pallas kernels, shards(): pl.pallas_call(back_kernel, grid=grid, in_specs=[block] * 5 + [tap_block,...  6.53 us
    pallas_call x1, Pallas kernels, shards(): pl.pallas_call(query_kernel, in_specs=[smem] + whole(2), out_specs=whole(...  6.11 us
    pallas_call x1, Pallas kernels, shards(): pl.pallas_call(key_kernel, in_specs=[smem] + whole(4 + ring), out_specs=w...  5.77 us
  transfers between devices with their start and end apart: 11, of which 0 were waited for; matrix products, arithmetic and copies ran while one was open for 7% of the time, Pallas kernels for 42%

profile of v4, /device:TPU:16, one launch (start us, length us, event | category | flops | bytes accessed | tf_op | source)
XLA Modules:
  0.0 180.8 jit_solution(4295141331148088780)
XLA Ops:
  7.2 0.0 all-gather.3.cloned.1.call-start
  7.2 2.0 %pack.1 = (bf16[4,2,128,128]{3,2,1,0:T(8,128)(2,1)}, bf16[4,2,128,128]{3,2,1,0:T(8,128)(2,1)}) custom-call(bf16[128,512]{1,0:T(8,128)(2,1)} %bitcast.50, bf16[128,512]{1,0:T(8,128)(2,1)} %bitcast.51, bf16[128,512]{1,0:T(8,128)(2,1)} %bitcast.52, bf16[128,512]{1,0:T(8,128)(2,1)} %bitcast.53), custom_call_target="tpu_custom_call" | custom-call | tf_op jit(solution)/shard_map/pack/pallas_call | solution.py:339
  9.2 16.2 %all_to_all.15.own_ref = bf16[4,2,128,128]{3,2,1,0:T(8,128)(2,1)} all-to-all(bf16[4,2,128,128]{3,2,1,0:T(8,128)(2,1)} %get-tuple-element.41), channel_id=1, replica_groups={{0,64,128,192},{8,72,136,200},{16,80,144,208},{24,88,152,216},{32,96,16..., dimensions={0} | all-to-all | bytes 524288 | tf_op jit(solution)/shard_map/all_to_all | solution.py:346
  25.5 0.0 all-gather.3.cloned.1.call-update
  25.5 11.2 %all_to_all.16.own_ref.refs_0_ = bf16[4,2,128,128]{3,2,1,0:T(8,128)(2,1)S(1)} all-to-all(bf16[4,2,128,128]{3,2,1,0:T(8,128)(2,1)} %get-tuple-element.43), channel_id=1, replica_groups={{0,64,128,192},{8,72,136,200},{16,80,144,208},{24,88,152,216},{32,96,16..., dimensions={0} | all-to-all | bytes 524288 | tf_op jit(solution)/shard_map/all_to_all | solution.py:349
  36.7 1.1 multiply_convert_fusion
  37.8 3.5 %collective-permute-start = (bf16[128,512]{1,0:T(8,128)(2,1)S(1)}, bf16[128,512]{1,0:T(8,128)(2,1)S(1)}, u32[]{:S(2)}, u32[]{:S(2)}) collective-permute-start(bf16[128,512]{1,0:T(8,128)(2,1)S(1)} %multiply_convert_fusion), channel_id=1, source_target_pairs={{0,8},{8,16},{16,24},{24,32},{32,40},{40,48},{48,56},{56,64},{64,7... | collective-permute-start | bytes 393224 | tf_op jit(solution)/shard_map/ppermute | solution.py:21
  41.3 4.7 %collective-permute-start.2 = (bf16[4,2,128,128]{3,2,1,0:T(8,128)(2,1)S(1)}, bf16[4,2,128,128]{3,2,1,0:T(8,128)(2,1)S(1)}, u32[]{:S(2)}, u32[]{:S(2)}) collective-permute-start(bf16[4,2,128,128]{3,2,1,0:T(8,128)(2,1)S(1)} %all_to_all.16.own_ref.refs_0_), channel_id=1, source_target_pairs={{0,8},{8,16},{16,24},{24,32},{32,40},{40,48},{48,56},{56,0},{64,72... | collective-permute-start | bytes 786440 | tf_op jit(solution)/shard_map/ppermute | solution.py:355
  46.0 2.7 %collective-permute-start.3 = (bf16[4,2,128,128]{3,2,1,0:T(8,128)(2,1)S(1)}, bf16[4,2,128,128]{3,2,1,0:T(8,128)(2,1)S(1)}, u32[]{:S(2)}, u32[]{:S(2)}) collective-permute-start(bf16[4,2,128,128]{3,2,1,0:T(8,128)(2,1)S(1)} %all_to_all.16.own_ref.refs_0_), channel_id=1, source_target_pairs={{0,16},{8,24},{16,32},{24,40},{32,48},{40,56},{48,0},{56,8},{64,80... | collective-permute-start | bytes 786440 | tf_op jit(solution)/shard_map/ppermute | solution.py:355
  48.8 0.9 copy.29.taps_ref
  49.6 0.7 copy-done.2
  50.3 4.6 %mix.1 = (f32[128,512]{1,0:T(8,128)}, f32[128,512]{1,0:T(8,128)}, f32[2,128,128]{2,1,0:T(8,128)}) custom-call(bf16[128,512]{1,0:T(8,128)(2,1)} %bitcast.40, bf16[128,512]{1,0:T(8,128)(2,1)} %bitcast.42, bf16[128,512]{1,0:T(8,128)(2,1)} %copy-done.2, bf16[128,512]{1,0:T(8,128)(2,1)} %bitcast.47, bf16[128,512]{1,0:T(8,128)(2,1)} %bitcast.54, ...), custom_call_target="tpu_custom_call" | custom-call | flops 16777216 | bytes 1310720 | tf_op jit(solution)/shard_map/mix/pallas_call | solution.py:370
  54.9 1.6 reduce_sum.18.refs_0_
  56.5 7.8 %tp_sums.1 = f32[2,128]{1,0:T(2,128)} custom-call(f32[2,128]{1,0:T(2,128)} %reduce_sum.18.refs_0_), custom_call_target="tpu_custom_call" | custom-call | tf_op jit(solution)/shard_map/tp_sums/pallas_call | solution.py:275
  64.3 1.3 copy.30
  65.7 2.1 %norm.1 = (bf16[128,512]{1,0:T(8,128)(2,1)}, bf16[128,512]{1,0:T(8,128)(2,1)}, bf16[128,512]{1,0:T(8,128)(2,1)}, bf16[128,512]{1,0:T(8,128)(2,1)}, f32[1,512]{1,0:T(1,128)}) custom-call(bf16[128,512]{1,0:T(8,128)(2,1)} %bitcast.46, bf16[128,512]{1,0:T(8,128)(2,1)} %bitcast.48, f32[128,512]{1,0:T(8,128)} %get-tuple-element.45.refs_2_, ...), custom_call_target="tpu_custom_call" | custom-call | flops 1310720 | bytes 1310720 | tf_op jit(solution)/shard_map/norm/pallas_call | solution.py:387
  67.8 3.2 %collective-permute-start.1 = (bf16[128,512]{1,0:T(8,128)(2,1)}, bf16[128,512]{1,0:T(8,128)(2,1)S(1)}, u32[]{:S(2)}, u32[]{:S(2)}) collective-permute-start(bf16[128,512]{1,0:T(8,128)(2,1)} %get-tuple-element.49.gated_ref), channel_id=1, source_target_pairs={{8,0},{16,8},{24,16},{32,24},{40,32},{48,40},{56,48},{64,56},{72,6... | collective-permute-start | bytes 393224 | tf_op jit(solution)/shard_map/ppermute | solution.py:21
  71.1 6.3 %collective-permute-start.4 = (bf16[4,2,128,128]{3,2,1,0:T(8,128)(2,1)S(1)}, bf16[4,2,128,128]{3,2,1,0:T(8,128)(2,1)S(1)}, u32[]{:S(2)}, u32[]{:S(2)}) collective-permute-start(bf16[4,2,128,128]{3,2,1,0:T(8,128)(2,1)S(1)} %all_to_all.16.own_ref.refs_0_), channel_id=1, source_target_pairs={{0,24},{8,32},{16,40},{24,48},{32,56},{40,0},{48,8},{56,16},{64,88... | collective-permute-start | bytes 786440 | tf_op jit(solution)/shard_map/ppermute | solution.py:355
  77.3 3.4 %collective-permute-start.5 = (bf16[4,2,128,128]{3,2,1,0:T(8,128)(2,1)S(1)}, bf16[4,2,128,128]{3,2,1,0:T(8,128)(2,1)S(1)}, u32[]{:S(2)}, u32[]{:S(2)}) collective-permute-start(bf16[4,2,128,128]{3,2,1,0:T(8,128)(2,1)S(1)} %all_to_all.16.own_ref.refs_0_), channel_id=1, source_target_pairs={{0,32},{8,40},{16,48},{24,56},{32,0},{40,8},{48,16},{56,24},{64,96... | collective-permute-start | bytes 786440 | tf_op jit(solution)/shard_map/ppermute | solution.py:355
  80.7 0.0 collective-permute-done.1.after_ref
  80.7 0.0 copy-start.4
  80.7 4.2 %collective-permute-start.6 = (bf16[4,2,128,128]{3,2,1,0:T(8,128)(2,1)S(1)}, bf16[4,2,128,128]{3,2,1,0:T(8,128)(2,1)S(1)}, u32[]{:S(2)}, u32[]{:S(2)}) collective-permute-start(bf16[4,2,128,128]{3,2,1,0:T(8,128)(2,1)S(1)} %all_to_all.16.own_ref.refs_0_), channel_id=1, source_target_pairs={{0,40},{8,48},{16,56},{24,0},{32,8},{40,16},{48,24},{56,32},{64,10... | collective-permute-start | bytes 786440 | tf_op jit(solution)/shard_map/ppermute | solution.py:355
  84.9 6.5 %back.1 = (bf16[128,512]{1,0:T(8,128)(2,1)}, bf16[128,512]{1,0:T(8,128)(2,1)}, f32[128,512]{1,0:T(8,128)}, f32[1,512]{1,0:T(1,128)}) custom-call(bf16[128,512]{1,0:T(8,128)(2,1)} %bitcast.41, bf16[128,512]{1,0:T(8,128)(2,1)} %bitcast.43, bf16[128,512]{1,0:T(8,128)(2,1)} %copy-done.2, bf16[128,512]{1,0:T(8,128)(2,1)} %get-tuple-element.49.gated_ref, ...), custom_call_target="tpu_custom_call" | custom-call | flops 33554432 | bytes 1310720 | tf_op jit(solution)/shard_map/back/pallas_call | solution.py:398
  91.5 1.2 convolution_bitcast_fusion
  92.7 4.1 %collective-permute-start.7 = (bf16[4,2,128,128]{3,2,1,0:T(8,128)(2,1)S(1)}, bf16[4,2,128,128]{3,2,1,0:T(8,128)(2,1)S(1)}, u32[]{:S(2)}, u32[]{:S(2)}) collective-permute-start(bf16[4,2,128,128]{3,2,1,0:T(8,128)(2,1)S(1)} %all_to_all.16.own_ref.refs_0_), channel_id=1, source_target_pairs={{0,48},{8,56},{16,0},{24,8},{32,16},{40,24},{48,32},{56,40},{64,11... | collective-permute-start | bytes 786440 | tf_op jit(solution)/shard_map/ppermute | solution.py:355
  96.8 0.0 collective-permute-done.3.refs_2_
  96.9 2.5 %collective-permute-start.8 = (bf16[4,2,128,128]{3,2,1,0:T(8,128)(2,1)S(1)}, bf16[4,2,128,128]{3,2,1,0:T(8,128)(2,1)S(1)}, u32[]{:S(2)}, u32[]{:S(2)}) collective-permute-start(bf16[4,2,128,128]{3,2,1,0:T(8,128)(2,1)S(1)} %all_to_all.16.own_ref.refs_0_), channel_id=1, source_target_pairs={{0,56},{8,0},{16,8},{24,16},{32,24},{40,32},{48,40},{56,48},{64,12... | collective-permute-start | bytes 786440 | tf_op jit(solution)/shard_map/ppermute | solution.py:355
  99.3 0.7 maximum_bitcast_fusion
  100.0 6.1 %query.1 = (bf16[4,128,128]{2,1,0:T(8,128)(2,1)}, bf16[4,128,128]{2,1,0:T(8,128)(2,1)}, f32[4,2,128]{2,1,0:T(2,128)}) custom-call(s32[1]{0:T(128)} %bitcast.19.place_ref, bf16[4,2,128,128]{3,2,1,0:T(8,128)(2,1)} %copy-done.3, bf16[8,4,2,128,128]{4,3,2,1,0:T(8,128)(2,1)} %bitcast.64), custom_call_target="tpu_custom_call" | custom-call | flops 1342177280 | bytes 3145728 | tf_op jit(solution)/shard_map/query/pallas_call | solution.py:430
  106.2 1.3 pad_maximum_fusion.refs_0_
  107.5 26.3 %ring_gather.1 = f32[8,48,128]{2,1,0:T(8,128)} custom-call(f32[48,128]{1,0:T(8,128)} %pad_maximum_fusion.refs_0_), custom_call_target="tpu_custom_call" | custom-call | tf_op jit(solution)/shard_map/ring_gather/pallas_call | solution.py:275
  133.8 1.4 slice.22
  135.2 0.0 collective-permute-done.6.refs_5_
  135.2 0.0 collective-permute-done.8.refs_7_
  135.2 0.6 copy-done.8
  135.9 0.1 copy-done.9
  136.0 0.1 copy-done.10
  136.1 0.1 copy-done.11
  136.2 0.1 copy-done.12
  136.3 5.8 %key.1 = bf16[4,4,128,128]{3,2,1,0:T(8,128)(2,1)} custom-call(s32[1]{0:T(128)} %bitcast.19.place_ref, bf16[4,2,128,128]{3,2,1,0:T(8,128)(2,1)} %all_to_all.15.own_ref, f32[8,4,2,128]{3,2,1,0:T(2,128)} %bitcast.55, bf16[4,128,128]{2,1,0:T(8,128)(2,1)} %get-tuple-element.62.att_ref, bf16[4,128,128]{2,1,0:T(8,128)(2,1)} %get-tuple-element.63.dq_ref, ...), custom_call_target="tpu_custom_call" | custom-call | flops 1342177280 | bytes 3145728 | tf_op jit(solution)/shard_map/key/pallas_call | solution.py:450
  142.0 4.3 %all-to-all-start.2 = ((bf16[4,4,128,128]{3,2,1,0:T(8,128)(2,1)}), bf16[4,4,128,128]{3,2,1,0:T(8,128)(2,1)S(1)}, u32[]{:S(2)}, u32[]{:S(2)}) async-start(bf16[4,4,128,128]{3,2,1,0:T(8,128)(2,1)} %key.1), calls=%async_computation.2 | async-start | bytes 1048576 | tf_op jit(solution)/shard_map/all_to_all | solution.py:462
  146.3 0.6 slice_reduce_fusion.refs_0_
  146.9 21.6 %strip_sums.1 = f32[40,128]{1,0:T(8,128)} custom-call(f32[40,128]{1,0:T(8,128)} %slice_reduce_fusion.refs_0_), custom_call_target="tpu_custom_call" | custom-call | tf_op jit(solution)/shard_map/strip_sums/pallas_call | solution.py:275
  168.6 1.3 slice.24
  169.9 1.3 slice_bitcast_fusion
  171.3 0.0 all-to-all-done.2.in_ref
  171.3 0.8 copy-done
  172.1 1.9 %unpack.1 = (bf16[128,512]{1,0:T(8,128)(2,1)}, bf16[128,512]{1,0:T(8,128)(2,1)}, bf16[128,512]{1,0:T(8,128)(2,1)}, bf16[128,512]{1,0:T(8,128)(2,1)}) custom-call(bf16[4,4,128,128]{3,2,1,0:T(8,128)(2,1)} %copy-done), custom_call_target="tpu_custom_call" | custom-call | tf_op jit(solution)/shard_map/unpack/pallas_call | solution.py:463
  (26 shorter events, 0.1 us)
Async XLA Ops:
  7.2 41.5 %copy-start.5 = (f32[32,128]{1,0:T(8,128)S(1)}, f32[32,128]{1,0:T(8,128)}, u32[]{:S(2)}) copy-start(f32[32,128]{1,0:T(8,128)} %param.16) | copy-start | bytes 49156
  7.2 92.9 %all-gather.3.cloned.1.call-start = ((), (), s32[]{:S(2)}) async-start(), calls=%async_computation.3 | async-start | bytes 2359296 | tf_op jit(solution)/shard_map/all_gather | solution.py:347
  36.7 60.1 %copy-start.3 = (bf16[4,2,128,128]{3,2,1,0:T(8,128)(2,1)}, bf16[4,2,128,128]{3,2,1,0:T(8,128)(2,1)S(1)}, u32[]{:S(2)}) copy-start(bf16[4,2,128,128]{3,2,1,0:T(8,128)(2,1)S(1)} %all_to_all.16.own_ref.refs_0_) | copy-start | bytes 786436
  37.8 11.8 %collective-permute-start = (bf16[128,512]{1,0:T(8,128)(2,1)S(1)}, bf16[128,512]{1,0:T(8,128)(2,1)S(1)}, u32[]{:S(2)}, u32[]{:S(2)}) collective-permute-start(bf16[128,512]{1,0:T(8,128)(2,1)S(1)} %multiply_convert_fusion), channel_id=1, source_target_pairs={{0,8},{8,16},{16,24},{24,32},{32,40},{40,48},{48,56},{56,64},{64,7... | collective-permute-start | bytes 393224 | tf_op jit(solution)/shard_map/ppermute | solution.py:21
  41.3 51.4 %collective-permute-start.2 = (bf16[4,2,128,128]{3,2,1,0:T(8,128)(2,1)S(1)}, bf16[4,2,128,128]{3,2,1,0:T(8,128)(2,1)S(1)}, u32[]{:S(2)}, u32[]{:S(2)}) collective-permute-start(bf16[4,2,128,128]{3,2,1,0:T(8,128)(2,1)S(1)} %all_to_all.16.own_ref.refs_0_), channel_id=1, source_target_pairs={{0,8},{8,16},{16,24},{24,32},{32,40},{40,48},{48,56},{56,0},{64,72... | collective-permute-start | bytes 786440 | tf_op jit(solution)/shard_map/ppermute | solution.py:355
  46.0 50.8 %collective-permute-start.3 = (bf16[4,2,128,128]{3,2,1,0:T(8,128)(2,1)S(1)}, bf16[4,2,128,128]{3,2,1,0:T(8,128)(2,1)S(1)}, u32[]{:S(2)}, u32[]{:S(2)}) collective-permute-start(bf16[4,2,128,128]{3,2,1,0:T(8,128)(2,1)S(1)} %all_to_all.16.own_ref.refs_0_), channel_id=1, source_target_pairs={{0,16},{8,24},{16,32},{24,40},{32,48},{40,56},{48,0},{56,8},{64,80... | collective-permute-start | bytes 786440 | tf_op jit(solution)/shard_map/ppermute | solution.py:355
  49.6 0.7 copy-start.2
  67.8 12.9 %collective-permute-start.1 = (bf16[128,512]{1,0:T(8,128)(2,1)}, bf16[128,512]{1,0:T(8,128)(2,1)S(1)}, u32[]{:S(2)}, u32[]{:S(2)}) collective-permute-start(bf16[128,512]{1,0:T(8,128)(2,1)} %get-tuple-element.49.gated_ref), channel_id=1, source_target_pairs={{8,0},{16,8},{24,16},{32,24},{40,32},{48,40},{56,48},{64,56},{72,6... | collective-permute-start | bytes 393224 | tf_op jit(solution)/shard_map/ppermute | solution.py:21
  71.1 64.1 %collective-permute-start.4 = (bf16[4,2,128,128]{3,2,1,0:T(8,128)(2,1)S(1)}, bf16[4,2,128,128]{3,2,1,0:T(8,128)(2,1)S(1)}, u32[]{:S(2)}, u32[]{:S(2)}) collective-permute-start(bf16[4,2,128,128]{3,2,1,0:T(8,128)(2,1)S(1)} %all_to_all.16.own_ref.refs_0_), channel_id=1, source_target_pairs={{0,24},{8,32},{16,40},{24,48},{32,56},{40,0},{48,8},{56,16},{64,88... | collective-permute-start | bytes 786440 | tf_op jit(solution)/shard_map/ppermute | solution.py:355
  77.3 57.8 %collective-permute-start.5 = (bf16[4,2,128,128]{3,2,1,0:T(8,128)(2,1)S(1)}, bf16[4,2,128,128]{3,2,1,0:T(8,128)(2,1)S(1)}, u32[]{:S(2)}, u32[]{:S(2)}) collective-permute-start(bf16[4,2,128,128]{3,2,1,0:T(8,128)(2,1)S(1)} %all_to_all.16.own_ref.refs_0_), channel_id=1, source_target_pairs={{0,32},{8,40},{16,48},{24,56},{32,0},{40,8},{48,16},{56,24},{64,96... | collective-permute-start | bytes 786440 | tf_op jit(solution)/shard_map/ppermute | solution.py:355
  80.7 4.2 %copy-start.4 = (bf16[128,512]{1,0:T(8,128)(2,1)}, bf16[128,512]{1,0:T(8,128)(2,1)S(1)}, u32[]{:S(2)}) copy-start(bf16[128,512]{1,0:T(8,128)(2,1)S(1)} %collective-permute-done.1.after_ref) | copy-start | bytes 393220
  80.7 54.5 %collective-permute-start.6 = (bf16[4,2,128,128]{3,2,1,0:T(8,128)(2,1)S(1)}, bf16[4,2,128,128]{3,2,1,0:T(8,128)(2,1)S(1)}, u32[]{:S(2)}, u32[]{:S(2)}) collective-permute-start(bf16[4,2,128,128]{3,2,1,0:T(8,128)(2,1)S(1)} %all_to_all.16.own_ref.refs_0_), channel_id=1, source_target_pairs={{0,40},{8,48},{16,56},{24,0},{32,8},{40,16},{48,24},{56,32},{64,10... | collective-permute-start | bytes 786440 | tf_op jit(solution)/shard_map/ppermute | solution.py:355
  92.7 13.5 %copy-start.6 = (bf16[4,2,128,128]{3,2,1,0:T(8,128)(2,1)}, bf16[4,2,128,128]{3,2,1,0:T(8,128)(2,1)S(1)}, u32[]{:S(2)}) copy-start(bf16[4,2,128,128]{3,2,1,0:T(8,128)(2,1)S(1)} %collective-permute-done.2.refs_1_) | copy-start | bytes 786436
  92.7 42.5 %collective-permute-start.7 = (bf16[4,2,128,128]{3,2,1,0:T(8,128)(2,1)S(1)}, bf16[4,2,128,128]{3,2,1,0:T(8,128)(2,1)S(1)}, u32[]{:S(2)}, u32[]{:S(2)}) collective-permute-start(bf16[4,2,128,128]{3,2,1,0:T(8,128)(2,1)S(1)} %all_to_all.16.own_ref.refs_0_), channel_id=1, source_target_pairs={{0,48},{8,56},{16,0},{24,8},{32,16},{40,24},{48,32},{56,40},{64,11... | collective-permute-start | bytes 786440 | tf_op jit(solution)/shard_map/ppermute | solution.py:355
  96.8 9.3 %copy-start.7 = (bf16[4,2,128,128]{3,2,1,0:T(8,128)(2,1)}, bf16[4,2,128,128]{3,2,1,0:T(8,128)(2,1)S(1)}, u32[]{:S(2)}) copy-start(bf16[4,2,128,128]{3,2,1,0:T(8,128)(2,1)S(1)} %collective-permute-done.3.refs_2_) | copy-start | bytes 786436
  96.9 38.4 %collective-permute-start.8 = (bf16[4,2,128,128]{3,2,1,0:T(8,128)(2,1)S(1)}, bf16[4,2,128,128]{3,2,1,0:T(8,128)(2,1)S(1)}, u32[]{:S(2)}, u32[]{:S(2)}) collective-permute-start(bf16[4,2,128,128]{3,2,1,0:T(8,128)(2,1)S(1)} %all_to_all.16.own_ref.refs_0_), channel_id=1, source_target_pairs={{0,56},{8,0},{16,8},{24,16},{32,24},{40,32},{48,40},{56,48},{64,12... | collective-permute-start | bytes 786440 | tf_op jit(solution)/shard_map/ppermute | solution.py:355
  135.2 0.7 copy-start.8
  135.2 0.8 copy-start.9
  135.2 0.9 copy-start.10
  135.2 1.0 copy-start.11
  135.2 1.0 copy-start.12
  136.2 10.1 %copy-start.1 = (f32[8,48,128]{2,1,0:T(8,128)S(1)}, f32[8,48,128]{2,1,0:T(8,128)}, u32[]{:S(2)}) copy-start(f32[8,48,128]{2,1,0:T(8,128)} %ring_gather.1) | copy-start | bytes 589828
  142.0 29.2 %all-to-all-start.2 = ((bf16[4,4,128,128]{3,2,1,0:T(8,128)(2,1)}), bf16[4,4,128,128]{3,2,1,0:T(8,128)(2,1)S(1)}, u32[]{:S(2)}, u32[]{:S(2)}) async-start(bf16[4,4,128,128]{3,2,1,0:T(8,128)(2,1)} %key.1), calls=%async_computation.2 | async-start | bytes 1048576 | tf_op jit(solution)/shard_map/all_to_all | solution.py:462
  171.3 0.8 copy-start
Sparse Core Ops, SparseCore 0:
  25.6 65.7 all-gather.2

commit v5 on v3

--- a/solution.py
+++ b/solution.py
@@ -415,14 +415,6 @@
         [filter_part.reshape(-1), skip_part.reshape(-1), gain_part.reshape(-1)]
     )
     small, own_qd = lax.optimization_barrier((small.reshape(-1, LANES), own_qd))
-    small = exchange(small, ring, over_ring, True, 1, "ring_sums")
-    small = exchange(
-        small, strips * lax.axis_size("dp"), over_strips, True, 2, "strip_sums"
-    ).reshape(-1)
-    small, own_kv = lax.optimization_barrier((small, own_kv))
-    cut = groups * taps
-    filter_sum = small[:cut].reshape(groups, taps)
-    skip_sum, gain_sum = (small[cut : cut + channels], small[cut + channels :])
 
     smem = pl.BlockSpec(memory_space=pltpu.SMEM)
     blocks = (heads, rows, HEAD_DIM)
@@ -441,7 +433,21 @@
         ),
         name="query",
     )(place, own_qd, all_kv)
-    all_stats = exchange(stats, ring, over_ring, False, 3, "stats")
+    lines = 2 * heads
+    gathered = exchange(
+        jnp.concatenate([stats.reshape(lines, rows), small], axis=0),
+        ring, over_ring, False, 1, "ring_gather",
+    )
+    all_stats = gathered[:, :lines].reshape(ring, heads, 2, rows)
+    small = exchange(
+        jnp.sum(gathered[:, lines:], axis=0),
+        strips * lax.axis_size("dp"), over_strips, True, 2, "strip_sums",
+    )
+    small, own_kv = lax.optimization_barrier((small, own_kv))
+    small = small.reshape(-1)
+    cut = groups * taps
+    filter_sum = small[:cut].reshape(groups, taps)
+    skip_sum, gain_sum = (small[cut : cut + channels], small[cut + channels :])
     back = pl.pallas_call(
         key_kernel,
         in_specs=[smem] + whole(5),

time: 158 us -> 154 us (0.975)
  Pallas kernels: 75.6 us -> 66.8 us
  other arithmetic: 2.93 us -> 5.16 us
    pallas_call x4 -> x3, Pallas kernels: 46.8 us -> 38 us  [exchange(): pl.pallas_call(lambda *refs: exchange_kernel(*refs, team=team, summed=sum...]
  transfers between devices with their start and end apart: 5 -> 5, of which waited for: 3 -> 3; matrix products, arithmetic and copies ran while one was open for 5% -> 7% of each run, Pallas kernels for 42% -> 38%
where the time goes in v5:
time: 154 us; the launch traced here: 153 us
  Pallas kernels  66.8 us (43%)
  blocking collectives  27.5 us (18%)
  waiting for transfers between devices  21.3 us (14%)
  between operations  14.2 us (9%)
  starting transfers between devices  9.48 us (6%)
  local copies, waits for them, and re-layouts  6.97 us (5%)
  other arithmetic  5.16 us (3%)
    pallas_call x3, Pallas kernels, exchange(): pl.pallas_call(lambda *refs: exchange_kernel(*refs, team=team, summed=sum...  38 us
    all_to_all x1, blocking collectives, shards(): lax.all_to_all(send_kv, 'ctx', 0, 0, axis_index_groups=across, tiled=True)  16.2 us
    all_to_all x1, blocking collectives, shards(): lax.all_to_all(send_qd, 'ctx', 0, 0, axis_index_groups=across, tiled=True)  11.2 us
    all_to_all x1, waiting for transfers between devices, shards(): lax.all_to_all(back, 'ctx', 0, 0, axis_index_groups=across, tiled=True)  10.8 us
    ppermute x2, waiting for transfers between devices, passed_along(): lax.ppermute(value, axis, [(source, source + steps) for source in range(i...  10.5 us
    pallas_call x1, Pallas kernels, shards(): pl.pallas_call(back_kernel, grid=grid, in_specs=[block] * 5 + [tap_block,...  6.49 us
    pallas_call x1, Pallas kernels, shards(): pl.pallas_call(query_kernel, in_specs=[smem] + whole(2), out_specs=whole(...  6.11 us
    ppermute x2, starting transfers between devices, passed_along(): lax.ppermute(value, axis, [(source, source + steps) for source in range(i...  5.93 us
  transfers between devices with their start and end apart: 5, of which 3 were waited for; matrix products, arithmetic and copies ran while one was open for 7% of the time, Pallas kernels for 38%

profile of v5, /device:TPU:16, one launch (start us, length us, event | category | flops | bytes accessed | tf_op | source)
XLA Modules:
  0.0 152.6 jit_solution(4558546309454986556)
XLA Ops:
  7.2 0.0 copy-start.1
  7.2 0.0 copy-start.2
  7.2 0.0 copy-start.6
  7.2 0.0 all-gather.5.cloned.1.call-start
  7.3 2.0 %pack.1 = (bf16[4,2,128,128]{3,2,1,0:T(8,128)(2,1)}, bf16[4,2,128,128]{3,2,1,0:T(8,128)(2,1)}) custom-call(bf16[128,512]{1,0:T(8,128)(2,1)} %bitcast.51, bf16[128,512]{1,0:T(8,128)(2,1)} %bitcast.52, bf16[128,512]{1,0:T(8,128)(2,1)} %bitcast.53, bf16[128,512]{1,0:T(8,128)(2,1)} %bitcast.54), custom_call_target="tpu_custom_call" | custom-call | tf_op jit(solution)/shard_map/pack/pallas_call | solution.py:336
  9.3 16.2 %all_to_all.15.own_ref = bf16[4,2,128,128]{3,2,1,0:T(8,128)(2,1)} all-to-all(bf16[4,2,128,128]{3,2,1,0:T(8,128)(2,1)} %get-tuple-element.41), channel_id=1, replica_groups={{0,64,128,192},{8,72,136,200},{16,80,144,208},{24,88,152,216},{32,96,16..., dimensions={0} | all-to-all | bytes 524288 | tf_op jit(solution)/shard_map/all_to_all | solution.py:343
  25.5 0.0 all-gather.5.cloned.1.call-update
  25.6 0.0 all-gather.7.cloned.1.call-start
  25.6 11.2 %all_to_all.16.own_ref = bf16[4,2,128,128]{3,2,1,0:T(8,128)(2,1)} all-to-all(bf16[4,2,128,128]{3,2,1,0:T(8,128)(2,1)} %get-tuple-element.43), channel_id=1, replica_groups={{0,64,128,192},{8,72,136,200},{16,80,144,208},{24,88,152,216},{32,96,16..., dimensions={0} | all-to-all | bytes 524288 | tf_op jit(solution)/shard_map/all_to_all | solution.py:346
  36.8 0.0 all-gather.7.cloned.1.call-update
  36.9 0.0 copy-done.1
  36.9 0.0 copy-done.2
  36.9 3.5 %collective-permute-start = (bf16[128,512]{1,0:T(8,128)(2,1)S(1)}, bf16[128,512]{1,0:T(8,128)(2,1)S(1)}, u32[]{:S(2)}, u32[]{:S(2)}) collective-permute-start(bf16[128,512]{1,0:T(8,128)(2,1)S(1)} %multiply_convert_fusion), channel_id=1, source_target_pairs={{0,8},{8,16},{16,24},{24,32},{32,40},{40,48},{48,56},{56,64},{64,7... | collective-permute-start | bytes 393224 | tf_op jit(solution)/shard_map/ppermute | solution.py:21
  40.4 0.0 copy-done.6
  40.5 0.8 copy.29.taps_ref
  41.3 5.1 %collective-permute-done.before_ref = bf16[128,512]{1,0:T(8,128)(2,1)S(1)} collective-permute-done((bf16[128,512]{1,0:T(8,128)(2,1)S(1)}, bf16[128,512]{1,0:T(8,128)(2,1)S(1)}, u32[]{:S(2)}, u32[]{:S(2)}) %collective-permute-start) | collective-permute-done | bytes 131104 | tf_op jit(solution)/shard_map/ppermute | solution.py:21
  46.4 0.0 copy-start.3
  46.4 0.7 copy-done.3
  47.1 4.6 %mix.1 = (f32[128,512]{1,0:T(8,128)}, f32[128,512]{1,0:T(8,128)}, f32[2,128,128]{2,1,0:T(8,128)}) custom-call(bf16[128,512]{1,0:T(8,128)(2,1)} %bitcast.41, bf16[128,512]{1,0:T(8,128)(2,1)} %bitcast.43, bf16[128,512]{1,0:T(8,128)(2,1)} %copy-done.3, bf16[128,512]{1,0:T(8,128)(2,1)} %bitcast.48, bf16[128,512]{1,0:T(8,128)(2,1)} %bitcast.55, ...), custom_call_target="tpu_custom_call" | custom-call | flops 16777216 | bytes 1310720 | tf_op jit(solution)/shard_map/mix/pallas_call | solution.py:362
  51.7 1.6 %reduce_sum.18.refs_0_ = f32[2,128]{1,0:T(2,128)} reduce(f32[2,128,128]{2,1,0:T(8,128)} %get-tuple-element.47, f32[]{:T(128)} %constant.28.clone.1), dimensions={2}, to_apply=%region_0.1 | reduce | flops 32512 | bytes 132100 | tf_op jit(solution)/shard_map/reduce_sum | solution.py:378
  53.2 7.8 %tp_sums.1 = f32[2,128]{1,0:T(2,128)} custom-call(f32[2,128]{1,0:T(2,128)} %reduce_sum.18.refs_0_), custom_call_target="tpu_custom_call" | custom-call | tf_op jit(solution)/shard_map/tp_sums/pallas_call | solution.py:272
  61.1 1.4 copy.30
  62.5 2.1 %norm.1 = (bf16[128,512]{1,0:T(8,128)(2,1)}, bf16[128,512]{1,0:T(8,128)(2,1)}, bf16[128,512]{1,0:T(8,128)(2,1)}, bf16[128,512]{1,0:T(8,128)(2,1)}, f32[1,512]{1,0:T(1,128)}) custom-call(bf16[128,512]{1,0:T(8,128)(2,1)} %bitcast.47, bf16[128,512]{1,0:T(8,128)(2,1)} %bitcast.49, f32[128,512]{1,0:T(8,128)} %get-tuple-element.45.refs_2_, ...), custom_call_target="tpu_custom_call" | custom-call | flops 1310720 | bytes 1310720 | tf_op jit(solution)/shard_map/norm/pallas_call | solution.py:379
  64.6 2.4 %collective-permute-start.1 = (bf16[128,512]{1,0:T(8,128)(2,1)}, bf16[128,512]{1,0:T(8,128)(2,1)S(1)}, u32[]{:S(2)}, u32[]{:S(2)}) collective-permute-start(bf16[128,512]{1,0:T(8,128)(2,1)} %get-tuple-element.49.gated_ref), channel_id=1, source_target_pairs={{8,0},{16,8},{24,16},{32,24},{40,32},{48,40},{56,48},{64,56},{72,6... | collective-permute-start | bytes 393224 | tf_op jit(solution)/shard_map/ppermute | solution.py:21
  67.1 5.4 %collective-permute-done.1.after_ref = bf16[128,512]{1,0:T(8,128)(2,1)S(1)} collective-permute-done((bf16[128,512]{1,0:T(8,128)(2,1)}, bf16[128,512]{1,0:T(8,128)(2,1)S(1)}, u32[]{:S(2)}, u32[]{:S(2)}) %collective-permute-start.1) | collective-permute-done | bytes 131104 | tf_op jit(solution)/shard_map/ppermute | solution.py:21
  72.4 0.0 copy-start.4
  72.5 0.7 copy-done.4
  73.1 6.5 %back.1 = (bf16[128,512]{1,0:T(8,128)(2,1)}, bf16[128,512]{1,0:T(8,128)(2,1)}, f32[128,512]{1,0:T(8,128)}, f32[1,512]{1,0:T(1,128)}) custom-call(bf16[128,512]{1,0:T(8,128)(2,1)} %bitcast.42, bf16[128,512]{1,0:T(8,128)(2,1)} %bitcast.44, bf16[128,512]{1,0:T(8,128)(2,1)} %copy-done.3, bf16[128,512]{1,0:T(8,128)(2,1)} %get-tuple-element.49.gated_ref, ...), custom_call_target="tpu_custom_call" | custom-call | flops 33554432 | bytes 1310720 | tf_op jit(solution)/shard_map/back/pallas_call | solution.py:390
  79.6 1.2 convolution_bitcast_fusion
  80.8 0.7 maximum_bitcast_fusion
  81.5 0.0 all-gather.5.cloned.1.call-done
  81.5 6.1 %query.1 = (bf16[4,128,128]{2,1,0:T(8,128)(2,1)}, bf16[4,128,128]{2,1,0:T(8,128)(2,1)}, f32[4,2,128]{2,1,0:T(2,128)}) custom-call(s32[1]{0:T(128)} %bitcast.19.place_ref, bf16[4,2,128,128]{3,2,1,0:T(8,128)(2,1)} %all_to_all.16.own_ref, bf16[8,4,2,128,128]{4,3,2,1,0:T(8,128)(2,1)} %bitcast.66), custom_call_target="tpu_custom_call" | custom-call | flops 1342177280 | bytes 3145728 | tf_op jit(solution)/shard_map/query/pallas_call | solution.py:422
  87.6 1.3 pad_maximum_fusion.refs_0_
  88.9 17.5 %ring_gather.1 = f32[8,48,128]{2,1,0:T(8,128)} custom-call(f32[48,128]{1,0:T(8,128)} %pad_maximum_fusion.refs_0_), custom_call_target="tpu_custom_call" | custom-call | tf_op jit(solution)/shard_map/ring_gather/pallas_call | solution.py:272
  106.5 1.4 slice.28
  107.8 1.5 %slice_reduce_fusion.refs_0_ = f32[40,128]{1,0:T(8,128)} fusion(f32[8,48,128]{2,1,0:T(8,128)} %ring_gather.1), kind=kLoop, calls=%fused_computation.2 | loop fusion | flops 35840 | bytes 184320 | tf_op jit(solution)/shard_map/reduce_sum | solution.py:443
  109.4 12.6 %strip_sums.1 = f32[40,128]{1,0:T(8,128)} custom-call(f32[40,128]{1,0:T(8,128)} %slice_reduce_fusion.refs_0_), custom_call_target="tpu_custom_call" | custom-call | tf_op jit(solution)/shard_map/strip_sums/pallas_call | solution.py:272
  122.0 0.0 all-gather.7.cloned.1.call-done
  122.0 0.0 copy-start.5
  122.0 5.5 %key.1 = bf16[4,4,128,128]{3,2,1,0:T(8,128)(2,1)} custom-call(s32[1]{0:T(128)} %bitcast.19.place_ref, bf16[4,2,128,128]{3,2,1,0:T(8,128)(2,1)} %all_to_all.15.own_ref, bf16[8,4,2,128,128]{4,3,2,1,0:T(8,128)(2,1)} %bitcast.65, f32[8,4,2,128]{3,2,1,0:T(2,128)} %bitcast.56, bf16[4,128,128]{2,1,0:T(8,128)(2,1)} %get-tuple-element.64.att_ref, ...), custom_call_target="tpu_custom_call" | custom-call | flops 1342177280 | bytes 3145728 | tf_op jit(solution)/shard_map/key/pallas_call | solution.py:451
  127.6 3.5 %all-to-all-start.2 = ((bf16[4,4,128,128]{3,2,1,0:T(8,128)(2,1)}), bf16[4,4,128,128]{3,2,1,0:T(8,128)(2,1)S(1)}, u32[]{:S(2)}, u32[]{:S(2)}) async-start(bf16[4,4,128,128]{3,2,1,0:T(8,128)(2,1)} %key.1), calls=%async_computation.2 | async-start | bytes 1048576 | tf_op jit(solution)/shard_map/all_to_all | solution.py:461
  131.1 0.0 copy-done.5
  131.1 0.6 slice.23
  131.7 0.6 slice_bitcast_fusion
  132.3 10.8 %all-to-all-done.2.in_ref = bf16[4,4,128,128]{3,2,1,0:T(8,128)(2,1)S(1)} async-done(((bf16[4,4,128,128]{3,2,1,0:T(8,128)(2,1)}), bf16[4,4,128,128]{3,2,1,0:T(8,128)(2,1)S(1)}, u32[]{:S(2)}, u32[]{:S(2)}) %all-to-all-start.2) | async-done | bytes 524320 | tf_op jit(solution)/shard_map/all_to_all | solution.py:461
  143.0 0.0 copy-start
  143.0 0.8 copy-done
  143.8 1.9 %unpack.1 = (bf16[128,512]{1,0:T(8,128)(2,1)}, bf16[128,512]{1,0:T(8,128)(2,1)}, bf16[128,512]{1,0:T(8,128)(2,1)}, bf16[128,512]{1,0:T(8,128)(2,1)}) custom-call(bf16[4,4,128,128]{3,2,1,0:T(8,128)(2,1)} %copy-done), custom_call_target="tpu_custom_call" | custom-call | tf_op jit(solution)/shard_map/unpack/pallas_call | solution.py:462
  (3 shorter events, 0.1 us)
Async XLA Ops:
  7.2 29.7 %copy-start.1 = (bf16[1,128,512]{2,1,0:T(8,128)(2,1)S(1)}, bf16[1,128,512]{2,1,0:T(8,128)(2,1)}, u32[]{:S(2)}) copy-start(bf16[1,128,512]{2,1,0:T(8,128)(2,1)} %param.12) | copy-start | bytes 393220
  7.2 29.7 %copy-start.2 = (bf16[1,128,512]{2,1,0:T(8,128)(2,1)S(1)}, bf16[1,128,512]{2,1,0:T(8,128)(2,1)}, u32[]{:S(2)}) copy-start(bf16[1,128,512]{2,1,0:T(8,128)(2,1)} %param.14) | copy-start | bytes 393220
  7.2 33.2 %copy-start.6 = (f32[32,128]{1,0:T(8,128)S(1)}, f32[32,128]{1,0:T(8,128)}, u32[]{:S(2)}) copy-start(f32[32,128]{1,0:T(8,128)} %param.16) | copy-start | bytes 49156
  7.2 74.3 %all-gather.5.cloned.1.call-start = ((), (), s32[]{:S(2)}) async-start(), calls=%async_computation.3 | async-start | bytes 2359296 | tf_op jit(solution)/shard_map/all_gather | solution.py:344
  25.6 96.5 %all-gather.7.cloned.1.call-start = ((), (), s32[]{:S(2)}) async-start(), calls=%async_computation.4 | async-start | bytes 2359296 | tf_op jit(solution)/shard_map/all_gather | solution.py:347
  36.9 9.5 %collective-permute-start = (bf16[128,512]{1,0:T(8,128)(2,1)S(1)}, bf16[128,512]{1,0:T(8,128)(2,1)S(1)}, u32[]{:S(2)}, u32[]{:S(2)}) collective-permute-start(bf16[128,512]{1,0:T(8,128)(2,1)S(1)} %multiply_convert_fusion), channel_id=1, source_target_pairs={{0,8},{8,16},{16,24},{24,32},{32,40},{40,48},{48,56},{56,64},{64,7... | collective-permute-start | bytes 393224 | tf_op jit(solution)/shard_map/ppermute | solution.py:21
  46.4 0.7 copy-start.3
  64.6 7.8 %collective-permute-start.1 = (bf16[128,512]{1,0:T(8,128)(2,1)}, bf16[128,512]{1,0:T(8,128)(2,1)S(1)}, u32[]{:S(2)}, u32[]{:S(2)}) collective-permute-start(bf16[128,512]{1,0:T(8,128)(2,1)} %get-tuple-element.49.gated_ref), channel_id=1, source_target_pairs={{8,0},{16,8},{24,16},{32,24},{40,32},{48,40},{56,48},{64,56},{72,6... | collective-permute-start | bytes 393224 | tf_op jit(solution)/shard_map/ppermute | solution.py:21
  72.4 0.7 copy-start.4
  122.0 9.0 %copy-start.5 = (f32[40,128]{1,0:T(8,128)S(1)}, f32[40,128]{1,0:T(8,128)}, u32[]{:S(2)}) copy-start(f32[40,128]{1,0:T(8,128)} %strip_sums.1) | copy-start | bytes 61444
  127.6 15.4 %all-to-all-start.2 = ((bf16[4,4,128,128]{3,2,1,0:T(8,128)(2,1)}), bf16[4,4,128,128]{3,2,1,0:T(8,128)(2,1)S(1)}, u32[]{:S(2)}, u32[]{:S(2)}) async-start(bf16[4,4,128,128]{3,2,1,0:T(8,128)(2,1)} %key.1), calls=%async_computation.2 | async-start | bytes 1048576 | tf_op jit(solution)/shard_map/all_to_all | solution.py:461
  143.0 0.8 copy-start
Sparse Core Ops, SparseCore 0:
  25.7 44.2 all-gather.4
  72.1 45.6 all-gather.6
